TPU v7x, 32 devices: a whole 2x2x4 slice. The times are simulated.
32 devices in a mesh: seq: 8 (over y, x, core), tensor: 4 (over z).
Axes of the slice: x: 2, y: 2, z: 4, core: 2. Of those that a mesh axis runs over, the one named last changes fastest.
Arguments:
- patches: bfloat16 [2048, 6144], P('seq', 'tensor'), may hold values from -60 to 60
- segment_ids: int32 [2048], replicated, may hold values from 0 to 3, never falling along the last dimension, each value on 1 to 768 neighbouring positions
- w_query: bfloat16 [6144, 1024], P('seq', 'tensor'), may hold values from -0.078125 to 0.078125
- w_key: bfloat16 [6144, 1024], P('seq', 'tensor'), may hold values from -0.078125 to 0.078125
- w_value: bfloat16 [6144, 1024], P('seq', 'tensor'), may hold values from -0.078125 to 0.078125
- w_out: bfloat16 [1024, 6144], P('seq', 'tensor'), may hold values from -0.1875 to 0.1875
Outputs:
- attended: bfloat16 [2048, 6144], P('seq', 'tensor')
Inputs may be any that keep to these rules, and one draw needn't show every extreme that they name: `segment_ids`: image ids never fall along the row; every image holds at most 768 patches and some image exactly that many.
All inputs are finite; a program needn't handle non-finite values.
Results may differ from a plain program's by a relative error of at most 0.012.
The roundings to bfloat16 on the way count: a program that leaves them out, or rounds other values in their place, can miss the bound.
Values may be sent and summed in bfloat16 or wider, within the bound.
No kernel may reach another device: no remote copies, remote signals or barrier semaphores. Data moves between devices by JAX's collectives and lax.ppermute only.
A program may use at most 64 MiB of HBM per device.

v0:
```python
import jax
import jax.numpy as jnp
from jax import lax
from jax.experimental import pallas as pl
from jax.experimental.pallas import tpu as pltpu
from jax.sharding import PartitionSpec as P

HS = 128
NEG = -1e30
BF16 = jnp.bfloat16
F32 = jnp.float32
ANY = pl.BlockSpec(memory_space=pl.ANY)
VMEM = pl.BlockSpec(memory_space=pltpu.VMEM)
SMEM = pl.BlockSpec(memory_space=pltpu.SMEM)


def reversed_bits(value, bits):
    return sum(((value >> k) & 1) << (bits - 1 - k) for k in range(bits))


def chip_at(position, chip, core, bits):
    return chip ^ jnp.where(core == 0, position, reversed_bits(position, bits))


def permute(x, axes, pairs):
    return lax.ppermute(x, axes, pairs)


def gather_chips(x, chips):
    bits = chips.bit_length() - 1
    pieces = [x]
    for k in range(bits):
        pairs = [
            (2 * c + j, 2 * (c ^ (1 << (bits - 1 - k if j else k))) + j)
            for c in range(chips)
            for j in range(2)
        ]
        for q in range(1 << k):
            pieces.append(permute(pieces[q], "seq", pairs))
    return pieces


def swap_cores(pieces, devices):
    pairs = [(s, s ^ 1) for s in range(devices)]
    return [permute(piece, "seq", pairs) for piece in pieces]


def line_gather(x, count):
    below, above = [x], [x]
    for k in range(1, count):
        up = [(i, i + 1) for i in range(k - 1, count - 1)]
        down = [(i + 1, i) for i in range(count - k)]
        below.append(permute(below[-1], "tensor", up))
        above.append(permute(above[-1], "tensor", down))
    return below, above


def place():
    seq = lax.axis_index("seq")
    return seq // 2, seq % 2, lax.axis_index("tensor")


def project_most(chips, count, steps):
    bits = chips.bit_length() - 1

    def kernel(*refs):
        mine, theirs = refs[:chips], refs[chips : 2 * chips]
        xs = refs[2 * chips : 2 * chips + 1 + 2 * steps]
        acc, x_full, w_full, w_sem, x_sem = refs[2 * chips + 1 + 2 * steps :]
        chip, core, at = place()
        rows = mine[0].shape[0]

        def w_copy(block, source):
            to = w_full.at[pl.ds(pl.multiple_of(block * rows, rows), rows)]
            return pltpu.make_async_copy(source, to, w_sem.at[block])

        for p in range(chips):
            w_copy(2 * chip_at(p, chip, core, bits) + core, mine[p]).start()
            w_copy(2 * chip_at(p, chip, 1 - core, bits) + 1 - core, theirs[p]).start()

        def x_copy(block, source):
            return pltpu.make_async_copy(source, x_full.at[block], x_sem.at[block])

        x_copy(at, xs[0]).start()
        for k in range(1, steps + 1):

            @pl.when(at >= k)
            def _():
                x_copy(at - k, xs[k]).start()

            @pl.when(at + k < count)
            def _():
                x_copy(at + k, xs[steps + k]).start()

        acc[...] = jnp.zeros(acc.shape, F32)
        depth = x_full.shape[2]
        per = depth // rows

        def step(block, _):
            for i in range(per):
                w_copy(block * per + i, mine[0]).wait()

            @pl.when(jnp.abs(block - at) <= steps)
            def _():
                x_copy(block, xs[0]).wait()
                w = w_full[pl.ds(pl.multiple_of(block * depth, depth), depth), :]
                acc[...] += jnp.dot(x_full[block], w, preferred_element_type=F32)

            return 0

        lax.fori_loop(0, count, step, 0)

    return kernel


def project_last(chips, count):
    bits = chips.bit_length() - 1

    def kernel(*refs):
        mine, theirs = refs[:chips], refs[chips : 2 * chips]
        acc_in, from_below, from_above, q_out, kv_out = refs[2 * chips : 2 * chips + 5]
        acc, x_block, w_block, w_sem, x_sem, acc_sem = refs[2 * chips + 5 :]
        chip, core, at = place()
        rows = mine[0].shape[0]
        get_acc = pltpu.make_async_copy(acc_in, acc, acc_sem)
        get_acc.start()
        edge = (at == 0) | (at == count - 1)

        def w_copy(kind, source):
            return pltpu.make_async_copy(source, w_block.at[pl.ds(pl.multiple_of(kind * rows, rows), rows)], w_sem.at[kind])

        def x_copy(source):
            return pltpu.make_async_copy(source, x_block, x_sem)

        @pl.when(at == 0)
        def _():
            x_copy(from_above).start()

        @pl.when(at == count - 1)
        def _():
            x_copy(from_below).start()

        wanted = jnp.where(at == 0, count - 1, 0)
        for p in range(chips):

            @pl.when(edge & (chip_at(p, chip, core, bits) == wanted))
            def _():
                w_copy(core, mine[p]).start()

            @pl.when(edge & (chip_at(p, chip, 1 - core, bits) == wanted))
            def _():
                w_copy(1 - core, theirs[p]).start()

        get_acc.wait()

        @pl.when(edge)
        def _():
            x_copy(from_below).wait()
            w_copy(0, mine[0]).wait()
            w_copy(1, mine[0]).wait()
            acc[...] += jnp.dot(x_block[...], w_block[...], preferred_element_type=F32)

        width = q_out.shape[1]
        q_out[...] = acc[:, :width].astype(BF16)
        kv_out[...] = acc[:, width:].astype(BF16)

    return kernel


def attend(chips):
    bits = chips.bit_length() - 1

    def kernel(ids, key_ids, q_ref, *refs):
        mine, theirs = refs[:chips], refs[chips : 2 * chips]
        out_ref, kv, sem = refs[2 * chips :]
        chip, core, _ = place()
        copies = []
        for p in range(chips):
            source = 2 * chip_at(p, chip, core, bits) + core
            copies.append(pltpu.make_async_copy(mine[p], kv.at[source], sem.at[2 * p]))
            source = 2 * chip_at(p, chip, 1 - core, bits) + 1 - core
            copies.append(pltpu.make_async_copy(theirs[p], kv.at[source], sem.at[2 * p + 1]))
        for copy in copies:
            copy.start()
        rows, width = q_ref.shape
        own = 2 * chip + core
        first, last = ids[own * rows], ids[own * rows + rows - 1]

        def count_out(block, carry):
            low, high = carry
            low += (ids[block * rows + rows - 1] < first).astype(jnp.int32)
            high -= (ids[block * rows] > last).astype(jnp.int32)
            return low, high

        low, high = lax.fori_loop(0, 2 * chips, count_out, (0, 2 * chips))
        row_ids = jnp.broadcast_to(key_ids[own], (128, rows)).T[:, :1]
        queries = [q_ref[:, h * HS : (h + 1) * HS] for h in range(2)]
        for copy in copies:
            copy.wait()

        def step(block, carry):
            here = kv[block]
            same = row_ids == key_ids[block]
            result = []
            for h, (top, total, out) in enumerate(carry):
                keys = here[:, h * HS : (h + 1) * HS]
                values = here[:, width + h * HS : width + (h + 1) * HS]
                scores = lax.dot_general(
                    queries[h], keys, (((1,), (1,)), ((), ())), preferred_element_type=F32
                ) * (HS**-0.5)
                scores = jnp.where(same, scores, NEG)
                new_top = jnp.maximum(top, jnp.max(scores, axis=1, keepdims=True))
                probs = jnp.exp(scores - new_top)
                fade = jnp.exp(top - new_top)
                total = total * fade + jnp.sum(probs, axis=1, keepdims=True)
                out = out * fade + jnp.dot(probs.astype(BF16), values, preferred_element_type=F32)
                result.append((new_top, total, out))
            return tuple(result)

        start = (jnp.full((rows, 1), NEG, F32), jnp.zeros((rows, 1), F32), jnp.zeros((rows, HS), F32))
        for h, (_, total, out) in enumerate(lax.fori_loop(low, high, step, (start, start))):
            out_ref[:, h * HS : (h + 1) * HS] = (out / total).astype(BF16)

    return kernel


def finish(chips, count):
    bits = chips.bit_length() - 1

    def kernel(*refs):
        mine, theirs = refs[:chips], refs[chips : 2 * chips]
        heads = refs[2 * chips : 2 * chips + count]
        out, w_full, h_full, sem = refs[2 * chips + count :]
        chip, core, at = place()
        rows = mine[0].shape[0]
        width = heads[0].shape[1]
        copies = []

        def w_copy(block, source):
            to = w_full.at[pl.ds(pl.multiple_of(block * rows, rows), rows)]
            copies.append(pltpu.make_async_copy(source, to, sem.at[len(copies)]))

        for p in range(chips):
            w_copy(2 * chip_at(p, chip, core, bits) + core, mine[p])
            w_copy(2 * chip_at(p, chip, 1 - core, bits) + 1 - core, theirs[p])
        for k in range(count):
            source = lax.rem(at - k + count, count)
            to = h_full.at[:, pl.ds(pl.multiple_of(source * width, width), width)]
            copies.append(pltpu.make_async_copy(heads[k], to, sem.at[len(copies)]))
        for copy in copies:
            copy.start()
        for copy in copies:
            copy.wait()
        out[...] = jnp.dot(h_full[...], w_full[...], preferred_element_type=F32).astype(BF16)

    return kernel


def call(kernel, *args, flops, read, exps=0, **settings):
    cost = pl.CostEstimate(flops=flops, bytes_accessed=read, transcendentals=exps)
    return pl.pallas_call(kernel, cost_estimate=cost, **settings)(*args)


def steps_on_device(patches, segment_ids, w_query, w_key, w_value, w_out):
    rows, depth = patches.shape
    devices, count = lax.axis_size("seq"), lax.axis_size("tensor")
    chips = devices // 2
    width = w_query.shape[1]
    assert width == 2 * HS and devices == 2 * count and w_out.shape[0] == HS
    dma = pltpu.SemaphoreType.DMA
    shape = jax.ShapeDtypeStruct
    cols = 3 * width
    steps = count - 2

    below, above = line_gather(patches, count)
    w_mine = gather_chips(jnp.concatenate([w_query, w_key, w_value], axis=1), chips)
    w_theirs = swap_cores(w_mine, devices)
    out_mine = gather_chips(w_out, chips)
    out_theirs = swap_cores(out_mine, devices)

    acc = call(
        project_most(chips, count, steps),
        *w_mine,
        *w_theirs,
        *below[: steps + 1],
        *above[1 : steps + 1],
        flops=2 * rows * cols * depth * count,
        read=2 * count * depth * (rows + cols),
        out_shape=shape((rows, cols), F32),
        in_specs=[ANY] * (2 * chips + 1 + 2 * steps),
        out_specs=VMEM,
        scratch_shapes=[
            pltpu.VMEM((count, rows, depth), BF16),
            pltpu.VMEM((count * depth, cols), BF16),
            dma((devices,)),
            dma((count,)),
        ],
    )
    queries, kv = call(
        project_last(chips, count),
        *w_mine,
        *w_theirs,
        acc,
        below[-1],
        above[-1],
        flops=2 * rows * cols * depth,
        read=2 * depth * (rows + cols) + 4 * rows * cols,
        out_shape=[shape((rows, width), BF16), shape((rows, 2 * width), BF16)],
        in_specs=[ANY] * (2 * chips + 3),
        out_specs=[VMEM] * 2,
        scratch_shapes=[
            pltpu.VMEM((rows, cols), F32),
            pltpu.VMEM((rows, depth), BF16),
            pltpu.VMEM((depth, cols), BF16),
            dma((2,)),
            dma(()),
            dma(()),
        ],
    )

    kv_mine = gather_chips(kv, chips)
    kv_theirs = swap_cores(kv_mine, devices)
    heads = call(
        attend(chips),
        segment_ids,
        segment_ids.reshape(devices, 1, rows),
        queries,
        *kv_mine,
        *kv_theirs,
        flops=8 * rows * rows * devices * HS,
        read=8 * rows * devices * HS,
        exps=2 * rows * rows * devices,
        out_shape=shape((rows, width), BF16),
        in_specs=[SMEM, VMEM, VMEM] + [ANY] * (2 * chips),
        out_specs=VMEM,
        scratch_shapes=[pltpu.VMEM((devices, rows, 2 * width), BF16), dma((devices,))],
    )

    all_heads = [heads]
    for k in range(1, count):
        all_heads.append(permute(heads, "tensor", [(z, (z + k) % count) for z in range(count)]))
    return call(
        finish(chips, count),
        *out_mine,
        *out_theirs,
        *all_heads,
        flops=2 * rows * devices * HS * w_out.shape[1],
        read=2 * devices * HS * (rows + w_out.shape[1]),
        out_shape=shape((rows, w_out.shape[1]), BF16),
        in_specs=[ANY] * (2 * chips + count),
        out_specs=VMEM,
        scratch_shapes=[
            pltpu.VMEM((devices * HS, w_out.shape[1]), BF16),
            pltpu.VMEM((rows, devices * HS), BF16),
            dma((2 * chips + count,)),
        ],
    )


def solution(mesh):
    spec = P("seq", "tensor")
    return jax.shard_map(
        steps_on_device, mesh=mesh, in_specs=(spec, P(), spec, spec, spec, spec), out_specs=spec, check_vma=False
    )
```

profile of v0, /device:TPU:0, one launch (start us, length us, event | category | flops | bytes accessed | tf_op | source)
XLA Modules:
  0.0 137.2 jit_solution(15574622670352325255)
XLA Ops:
  0.0 1.1 constant_dynamic-update-slice_fusion.2
  1.1 1.0 constant_dynamic-update-slice_fusion.1
  2.2 3.0 %collective-permute-start.7 = (bf16[768,768]{1,0:T(8,128)(2,1)S(1)}, bf16[768,768]{1,0:T(8,128)(2,1)S(1)}, u32[]{:S(2)}, u32[]{:S(2)}) collective-permute-start(bf16[768,768]{1,0:T(8,128)(2,1)S(1)} %constant_dynamic-update-slice_fusion.refs_0_), channel_id=1, source_target_pairs={{0,8},{4,20},{8,0},{12,28},{16,24},{20,4},{24,16},{28,12},{1,9},{5... | collective-permute-start | bytes 3538952 | tf_op jit(solution)/shard_map/ppermute | solution.py:26
  5.2 1.5 %collective-permute-start.8 = (bf16[768,768]{1,0:T(8,128)(2,1)S(1)}, bf16[768,768]{1,0:T(8,128)(2,1)S(1)}, u32[]{:S(2)}, u32[]{:S(2)}) collective-permute-start(bf16[768,768]{1,0:T(8,128)(2,1)S(1)} %constant_dynamic-update-slice_fusion.refs_0_), channel_id=1, source_target_pairs={{0,16},{4,12},{8,24},{12,4},{16,0},{20,28},{24,8},{28,20},{1,17},{... | collective-permute-start | bytes 3538952 | tf_op jit(solution)/shard_map/ppermute | solution.py:26
  6.8 24.7 %collective-permute-done.7.refs_1_ = bf16[768,768]{1,0:T(8,128)(2,1)S(1)} collective-permute-done((bf16[768,768]{1,0:T(8,128)(2,1)S(1)}, bf16[768,768]{1,0:T(8,128)(2,1)S(1)}, u32[]{:S(2)}, u32[]{:S(2)}) %collective-permute-start.7) | collective-permute-done | bytes 1179680 | tf_op jit(solution)/shard_map/ppermute | solution.py:26
  31.5 1.6 %collective-permute-start.9 = (bf16[768,768]{1,0:T(8,128)(2,1)S(1)}, bf16[768,768]{1,0:T(8,128)(2,1)S(1)}, u32[]{:S(2)}, u32[]{:S(2)}) collective-permute-start(bf16[768,768]{1,0:T(8,128)(2,1)S(1)} %collective-permute-done.7.refs_1_), channel_id=1, source_target_pairs={{0,16},{4,12},{8,24},{12,4},{16,0},{20,28},{24,8},{28,20},{1,17},{... | collective-permute-start | bytes 3538952 | tf_op jit(solution)/shard_map/ppermute | solution.py:26
  33.1 3.7 %collective-permute-start.14 = (bf16[256,1536]{1,0:T(8,128)(2,1)S(1)}, bf16[256,1536]{1,0:T(8,128)(2,1)S(1)}, u32[]{:S(2)}, u32[]{:S(2)}) collective-permute-start(bf16[256,1536]{1,0:T(8,128)(2,1)S(1)} %copy-done.7), channel_id=1, source_target_pairs={{0,1},{1,2},{2,3},{4,5},{5,6},{6,7},{8,9},{9,10},{10,11},{12,13},{... | collective-permute-start | bytes 2359304 | tf_op jit(solution)/shard_map/ppermute | solution.py:26
  36.7 1.3 collective-permute-start.16
  38.0 13.5 %collective-permute-done.14.refs_9_ = bf16[256,1536]{1,0:T(8,128)(2,1)S(1)} collective-permute-done((bf16[256,1536]{1,0:T(8,128)(2,1)S(1)}, bf16[256,1536]{1,0:T(8,128)(2,1)S(1)}, u32[]{:S(2)}, u32[]{:S(2)}) %collective-permute-start.14) | collective-permute-done | bytes 786464 | tf_op jit(solution)/shard_map/ppermute | solution.py:26
  51.5 1.6 %collective-permute-start.15 = (bf16[256,1536]{1,0:T(8,128)(2,1)S(1)}, bf16[256,1536]{1,0:T(8,128)(2,1)}, u32[]{:S(2)}, u32[]{:S(2)}) collective-permute-start(bf16[256,1536]{1,0:T(8,128)(2,1)S(1)} %collective-permute-done.14.refs_9_), channel_id=1, source_target_pairs={{1,2},{2,3},{5,6},{6,7},{9,10},{10,11},{13,14},{14,15},{17,18},{18... | collective-permute-start | bytes 2359304 | tf_op jit(solution)/shard_map/ppermute | solution.py:26
  53.1 2.6 %collective-permute-done.16.refs_11_ = bf16[256,1536]{1,0:T(8,128)(2,1)S(1)} collective-permute-done((bf16[256,1536]{1,0:T(8,128)(2,1)S(1)}, bf16[256,1536]{1,0:T(8,128)(2,1)S(1)}, u32[]{:S(2)}, u32[]{:S(2)}) %collective-permute-start.16) | collective-permute-done | bytes 786464 | tf_op jit(solution)/shard_map/ppermute | solution.py:26
  55.7 1.3 collective-permute-start.17
  57.0 0.0 collective-permute-done.8.refs_2_
  57.0 0.1 collective-permute-start.11
  57.1 0.0 collective-permute-done.10.refs_4_
  57.1 0.5 collective-permute-start.12
  57.6 0.0 collective-permute-done.9.refs_3_
  57.6 0.1 collective-permute-start.13
  57.7 1.6 %collective-permute-start.18 = (bf16[256,1536]{1,0:T(8,128)(2,1)}, bf16[256,1536]{1,0:T(8,128)(2,1)}, u32[]{:S(2)}, u32[]{:S(2)}) collective-permute-start(bf16[256,1536]{1,0:T(8,128)(2,1)} %collective-permute-done.15.refs_10_), channel_id=1, source_target_pairs={{2,3},{6,7},{10,11},{14,15},{18,19},{22,23},{26,27},{30,31}} | collective-permute-start | bytes 2359304 | tf_op jit(solution)/shard_map/ppermute | solution.py:26
  59.3 15.6 %collective-permute-done.17.refs_12_ = bf16[256,1536]{1,0:T(8,128)(2,1)} collective-permute-done((bf16[256,1536]{1,0:T(8,128)(2,1)S(1)}, bf16[256,1536]{1,0:T(8,128)(2,1)}, u32[]{:S(2)}, u32[]{:S(2)}) %collective-permute-start.17) | collective-permute-done | bytes 786464 | tf_op jit(solution)/shard_map/ppermute | solution.py:26
  74.9 1.3 collective-permute-start.19
  76.2 0.1 collective-permute-start
  76.3 1.8 %collective-permute-start.1 = (bf16[128,1536]{1,0:T(8,128)(2,1)}, bf16[128,1536]{1,0:T(8,128)(2,1)}, u32[]{:S(2)}, u32[]{:S(2)}) collective-permute-start(bf16[128,1536]{1,0:T(8,128)(2,1)} %refs_0_.1), channel_id=1, source_target_pairs={{0,16},{4,12},{8,24},{12,4},{16,0},{20,28},{24,8},{28,20},{1,17},{... | collective-permute-start | bytes 1179656 | tf_op jit(solution)/shard_map/ppermute | solution.py:26
  78.2 6.2 %shard_map.64.refs_8_ = f32[256,768]{1,0:T(8,128)} custom-call(bf16[768,768]{1,0:T(8,128)(2,1)} %copy-done, bf16[768,768]{1,0:T(8,128)(2,1)} %copy-done.1, bf16[768,768]{1,0:T(8,128)(2,1)} %copy-done.2, bf16[768,768]{1,0:T(8,128)(2,1)} %copy-done.4, bf16[768,768]{1,0:T(8,128)(2,1)} %copy-done.3, bf16[768,768]{1,0:T(8,128)(2,1)} %copy-done.5, ...), custom_call_target="tpu_custom_call" | custom-call | flops 2415919104 | bytes 12582912 | tf_op jit(solution)/shard_map/pallas_call | solution.py:261
  84.4 8.3 %collective-permute-done.19.refs_10_ = bf16[256,1536]{1,0:T(8,128)(2,1)} collective-permute-done((bf16[256,1536]{1,0:T(8,128)(2,1)}, bf16[256,1536]{1,0:T(8,128)(2,1)}, u32[]{:S(2)}, u32[]{:S(2)}) %collective-permute-start.19) | collective-permute-done | bytes 786464 | tf_op jit(solution)/shard_map/ppermute | solution.py:26
  92.7 3.7 %shard_map.65 = (bf16[256,256]{1,0:T(8,128)(2,1)}, bf16[256,512]{1,0:T(8,128)(2,1)}) custom-call(bf16[768,768]{1,0:T(8,128)(2,1)} %copy-done, bf16[768,768]{1,0:T(8,128)(2,1)} %copy-done.1, bf16[768,768]{1,0:T(8,128)(2,1)} %copy-done.2, bf16[768,768]{1,0:T(8,128)(2,1)} %copy-done.4, bf16[768,768]{1,0:T(8,128)(2,1)} %copy-done.3, bf16[768,768]{1,0:T(8,128)(2,1)} %copy-done.5, ...), custom_call_target="tpu_custom_call" | custom-call | flops 603979776 | bytes 3932160 | tf_op jit(solution)/shard_map/pallas_call | solution.py:261
  96.4 0.1 collective-permute-start.20
  96.5 2.0 %collective-permute-start.21 = (bf16[256,512]{1,0:T(8,128)(2,1)}, bf16[256,512]{1,0:T(8,128)(2,1)S(1)}, u32[]{:S(2)}, u32[]{:S(2)}) collective-permute-start(bf16[256,512]{1,0:T(8,128)(2,1)} %get-tuple-element.8.refs_0_), channel_id=1, source_target_pairs={{0,16},{4,12},{8,24},{12,4},{16,0},{20,28},{24,8},{28,20},{1,17},{... | collective-permute-start | bytes 786440 | tf_op jit(solution)/shard_map/ppermute | solution.py:26
  98.5 0.1 collective-permute-start.2
  98.6 7.3 %collective-permute-done.20.refs_1_ = bf16[256,512]{1,0:T(8,128)(2,1)S(1)} collective-permute-done((bf16[256,512]{1,0:T(8,128)(2,1)}, bf16[256,512]{1,0:T(8,128)(2,1)S(1)}, u32[]{:S(2)}, u32[]{:S(2)}) %collective-permute-start.20) | collective-permute-done | bytes 262176 | tf_op jit(solution)/shard_map/ppermute | solution.py:26
  105.9 1.9 %collective-permute-start.22 = (bf16[256,512]{1,0:T(8,128)(2,1)S(1)}, bf16[256,512]{1,0:T(8,128)(2,1)S(1)}, u32[]{:S(2)}, u32[]{:S(2)}) collective-permute-start(bf16[256,512]{1,0:T(8,128)(2,1)S(1)} %collective-permute-done.20.refs_1_), channel_id=1, source_target_pairs={{0,16},{4,12},{8,24},{12,4},{16,0},{20,28},{24,8},{28,20},{1,17},{... | collective-permute-start | bytes 786440 | tf_op jit(solution)/shard_map/ppermute | solution.py:26
  107.8 0.5 collective-permute-start.25
  108.3 0.1 collective-permute-start.3
  108.4 0.4 collective-permute-start.4
  108.8 3.4 %collective-permute-done.22.refs_3_ = bf16[256,512]{1,0:T(8,128)(2,1)S(1)} collective-permute-done((bf16[256,512]{1,0:T(8,128)(2,1)S(1)}, bf16[256,512]{1,0:T(8,128)(2,1)S(1)}, u32[]{:S(2)}, u32[]{:S(2)}) %collective-permute-start.22) | collective-permute-done | bytes 262176 | tf_op jit(solution)/shard_map/ppermute | solution.py:26
  112.2 0.5 collective-permute-start.5
  112.7 0.1 collective-permute-start.6
  112.8 0.9 collective-permute-done.26.refs_7_
  113.8 0.7 copy-done.22
  114.5 5.0 %shard_map.66.refs_8_ = bf16[256,256]{1,0:T(8,128)(2,1)} custom-call(s32[2048]{0:T(1024)} %ids.1, s32[8,1,256]{2,1,0:T(1,128)} %bitcast.1, bf16[256,256]{1,0:T(8,128)(2,1)} %get-tuple-element.7.q_ref, bf16[256,512]{1,0:T(8,128)(2,1)} %get-tuple-element.8.refs_0_, bf16[256,512]{1,0:T(8,128)(2,1)} %copy-done.16, bf16[256,512]{1,0:T(8,128)(2,1)} %copy-done.17, ...), custom_call_target="tpu_custom_call" | custom-call | flops 536870912 | bytes 2097152 | tf_op jit(solution)/shard_map/pallas_call | solution.py:261
  119.5 0.1 collective-permute-start.27
  119.6 0.2 collective-permute-start.28
  119.8 3.7 %collective-permute-start.29 = (bf16[256,256]{1,0:T(8,128)(2,1)}, bf16[256,256]{1,0:T(8,128)(2,1)S(1)}, u32[]{:S(2)}, u32[]{:S(2)}) collective-permute-start(bf16[256,256]{1,0:T(8,128)(2,1)} %shard_map.66.refs_8_), channel_id=1, source_target_pairs={{0,3},{1,0},{2,1},{3,2},{4,7},{5,4},{6,5},{7,6},{8,11},{9,8},{10,9... | collective-permute-start | bytes 393224 | tf_op jit(solution)/shard_map/ppermute | solution.py:26
  123.5 3.9 %collective-permute-done.27.refs_9_ = bf16[256,256]{1,0:T(8,128)(2,1)S(1)} collective-permute-done((bf16[256,256]{1,0:T(8,128)(2,1)}, bf16[256,256]{1,0:T(8,128)(2,1)S(1)}, u32[]{:S(2)}, u32[]{:S(2)}) %collective-permute-start.27) | collective-permute-done | bytes 131104 | tf_op jit(solution)/shard_map/ppermute | solution.py:26
  127.3 4.6 %collective-permute-done.28.refs_10_ = bf16[256,256]{1,0:T(8,128)(2,1)S(1)} collective-permute-done((bf16[256,256]{1,0:T(8,128)(2,1)}, bf16[256,256]{1,0:T(8,128)(2,1)S(1)}, u32[]{:S(2)}, u32[]{:S(2)}) %collective-permute-start.28) | collective-permute-done | bytes 131104 | tf_op jit(solution)/shard_map/ppermute | solution.py:26
  132.0 0.6 copy-done.24
  132.6 0.7 copy-done.25
  133.3 3.9 %shard_map.67 = bf16[256,1536]{1,0:T(8,128)(2,1)} custom-call(bf16[128,1536]{1,0:T(8,128)(2,1)} %refs_0_.1, bf16[128,1536]{1,0:T(8,128)(2,1)} %collective-permute-done.refs_1_, bf16[128,1536]{1,0:T(8,128)(2,1)} %collective-permute-done.1.refs_2_, bf16[128,1536]{1,0:T(8,128)(2,1)} %copy-done.10, bf16[128,1536]{1,0:T(8,128)(2,1)} %copy-done.11, ...), custom_call_target="tpu_custom_call" | custom-call | flops 805306368 | bytes 3670016 | tf_op jit(solution)/shard_map/pallas_call | solution.py:261
  (71 shorter events, 0.2 us)
Async XLA Ops:
  0.0 33.1 %copy-start.7 = (bf16[256,1536]{1,0:T(8,128)(2,1)S(1)}, bf16[256,1536]{1,0:T(8,128)(2,1)}, u32[]{:S(2)}) copy-start(bf16[256,1536]{1,0:T(8,128)(2,1)} %refs_8_.1) | copy-start | bytes 2359300
  2.2 75.9 %copy-start = (bf16[768,768]{1,0:T(8,128)(2,1)}, bf16[768,768]{1,0:T(8,128)(2,1)S(1)}, u32[]{:S(2)}) copy-start(bf16[768,768]{1,0:T(8,128)(2,1)S(1)} %constant_dynamic-update-slice_fusion.refs_0_) | copy-start | bytes 3538948
  2.2 29.3 %collective-permute-start.7 = (bf16[768,768]{1,0:T(8,128)(2,1)S(1)}, bf16[768,768]{1,0:T(8,128)(2,1)S(1)}, u32[]{:S(2)}, u32[]{:S(2)}) collective-permute-start(bf16[768,768]{1,0:T(8,128)(2,1)S(1)} %constant_dynamic-update-slice_fusion.refs_0_), channel_id=1, source_target_pairs={{0,8},{4,20},{8,0},{12,28},{16,24},{20,4},{24,16},{28,12},{1,9},{5... | collective-permute-start | bytes 3538952 | tf_op jit(solution)/shard_map/ppermute | solution.py:26
  5.2 51.8 %collective-permute-start.8 = (bf16[768,768]{1,0:T(8,128)(2,1)S(1)}, bf16[768,768]{1,0:T(8,128)(2,1)S(1)}, u32[]{:S(2)}, u32[]{:S(2)}) collective-permute-start(bf16[768,768]{1,0:T(8,128)(2,1)S(1)} %constant_dynamic-update-slice_fusion.refs_0_), channel_id=1, source_target_pairs={{0,16},{4,12},{8,24},{12,4},{16,0},{20,28},{24,8},{28,20},{1,17},{... | collective-permute-start | bytes 3538952 | tf_op jit(solution)/shard_map/ppermute | solution.py:26
  6.8 50.3 %collective-permute-start.10 = (bf16[768,768]{1,0:T(8,128)(2,1)S(1)}, bf16[768,768]{1,0:T(8,128)(2,1)S(1)}, u32[]{:S(2)}, u32[]{:S(2)}) collective-permute-start(bf16[768,768]{1,0:T(8,128)(2,1)S(1)} %constant_dynamic-update-slice_fusion.refs_0_), channel_id=1, source_target_pairs={{0,4},{4,0},{8,12},{12,8},{16,20},{20,16},{24,28},{28,24},{1,5},{5... | collective-permute-start | bytes 3538952 | tf_op jit(solution)/shard_map/ppermute | solution.py:26
  31.5 46.6 %copy-start.1 = (bf16[768,768]{1,0:T(8,128)(2,1)}, bf16[768,768]{1,0:T(8,128)(2,1)S(1)}, u32[]{:S(2)}) copy-start(bf16[768,768]{1,0:T(8,128)(2,1)S(1)} %collective-permute-done.7.refs_1_) | copy-start | bytes 3538948
  31.5 26.1 %collective-permute-start.9 = (bf16[768,768]{1,0:T(8,128)(2,1)S(1)}, bf16[768,768]{1,0:T(8,128)(2,1)S(1)}, u32[]{:S(2)}, u32[]{:S(2)}) collective-permute-start(bf16[768,768]{1,0:T(8,128)(2,1)S(1)} %collective-permute-done.7.refs_1_), channel_id=1, source_target_pairs={{0,16},{4,12},{8,24},{12,4},{16,0},{20,28},{24,8},{28,20},{1,17},{... | collective-permute-start | bytes 3538952 | tf_op jit(solution)/shard_map/ppermute | solution.py:26
  33.1 18.5 %collective-permute-start.14 = (bf16[256,1536]{1,0:T(8,128)(2,1)S(1)}, bf16[256,1536]{1,0:T(8,128)(2,1)S(1)}, u32[]{:S(2)}, u32[]{:S(2)}) collective-permute-start(bf16[256,1536]{1,0:T(8,128)(2,1)S(1)} %copy-done.7), channel_id=1, source_target_pairs={{0,1},{1,2},{2,3},{4,5},{5,6},{6,7},{8,9},{9,10},{10,11},{12,13},{... | collective-permute-start | bytes 2359304 | tf_op jit(solution)/shard_map/ppermute | solution.py:26
  36.7 19.0 %collective-permute-start.16 = (bf16[256,1536]{1,0:T(8,128)(2,1)S(1)}, bf16[256,1536]{1,0:T(8,128)(2,1)S(1)}, u32[]{:S(2)}, u32[]{:S(2)}) collective-permute-start(bf16[256,1536]{1,0:T(8,128)(2,1)S(1)} %copy-done.7), channel_id=1, source_target_pairs={{1,0},{2,1},{3,2},{5,4},{6,5},{7,6},{9,8},{10,9},{11,10},{13,12},{... | collective-permute-start | bytes 2359304 | tf_op jit(solution)/shard_map/ppermute | solution.py:26
  51.5 26.6 %copy-start.8 = (bf16[256,1536]{1,0:T(8,128)(2,1)}, bf16[256,1536]{1,0:T(8,128)(2,1)S(1)}, u32[]{:S(2)}) copy-start(bf16[256,1536]{1,0:T(8,128)(2,1)S(1)} %collective-permute-done.14.refs_9_) | copy-start | bytes 2359300
  51.5 6.2 %collective-permute-start.15 = (bf16[256,1536]{1,0:T(8,128)(2,1)S(1)}, bf16[256,1536]{1,0:T(8,128)(2,1)}, u32[]{:S(2)}, u32[]{:S(2)}) collective-permute-start(bf16[256,1536]{1,0:T(8,128)(2,1)S(1)} %collective-permute-done.14.refs_9_), channel_id=1, source_target_pairs={{1,2},{2,3},{5,6},{6,7},{9,10},{10,11},{13,14},{14,15},{17,18},{18... | collective-permute-start | bytes 2359304 | tf_op jit(solution)/shard_map/ppermute | solution.py:26
  55.7 22.4 %copy-start.9 = (bf16[256,1536]{1,0:T(8,128)(2,1)}, bf16[256,1536]{1,0:T(8,128)(2,1)S(1)}, u32[]{:S(2)}) copy-start(bf16[256,1536]{1,0:T(8,128)(2,1)S(1)} %collective-permute-done.16.refs_11_) | copy-start | bytes 2359300
  55.7 19.2 %collective-permute-start.17 = (bf16[256,1536]{1,0:T(8,128)(2,1)S(1)}, bf16[256,1536]{1,0:T(8,128)(2,1)}, u32[]{:S(2)}, u32[]{:S(2)}) collective-permute-start(bf16[256,1536]{1,0:T(8,128)(2,1)S(1)} %collective-permute-done.16.refs_11_), channel_id=1, source_target_pairs={{1,0},{2,1},{5,4},{6,5},{9,8},{10,9},{13,12},{14,13},{17,16},{18,1... | collective-permute-start | bytes 2359304 | tf_op jit(solution)/shard_map/ppermute | solution.py:26
  57.0 21.1 %copy-start.2 = (bf16[768,768]{1,0:T(8,128)(2,1)}, bf16[768,768]{1,0:T(8,128)(2,1)S(1)}, u32[]{:S(2)}) copy-start(bf16[768,768]{1,0:T(8,128)(2,1)S(1)} %collective-permute-done.8.refs_2_) | copy-start | bytes 3538948
  57.0 19.2 %collective-permute-start.11 = (bf16[768,768]{1,0:T(8,128)(2,1)S(1)}, bf16[768,768]{1,0:T(8,128)(2,1)S(1)}, u32[]{:S(2)}, u32[]{:S(2)}) collective-permute-start(bf16[768,768]{1,0:T(8,128)(2,1)S(1)} %collective-permute-done.7.refs_1_), channel_id=1, source_target_pairs={{0,4},{4,0},{8,12},{12,8},{16,20},{20,16},{24,28},{28,24},{1,5},{5... | collective-permute-start | bytes 3538952 | tf_op jit(solution)/shard_map/ppermute | solution.py:26
  57.1 19.2 %copy-start.3 = (bf16[768,768]{1,0:T(8,128)(2,1)}, bf16[768,768]{1,0:T(8,128)(2,1)S(1)}, u32[]{:S(2)}) copy-start(bf16[768,768]{1,0:T(8,128)(2,1)S(1)} %collective-permute-done.10.refs_4_) | copy-start | bytes 3538948
  57.1 19.2 %collective-permute-start.12 = (bf16[768,768]{1,0:T(8,128)(2,1)S(1)}, bf16[768,768]{1,0:T(8,128)(2,1)S(1)}, u32[]{:S(2)}, u32[]{:S(2)}) collective-permute-start(bf16[768,768]{1,0:T(8,128)(2,1)S(1)} %collective-permute-done.8.refs_2_), channel_id=1, source_target_pairs={{0,4},{4,0},{8,12},{12,8},{16,20},{20,16},{24,28},{28,24},{1,5},{5... | collective-permute-start | bytes 3538952 | tf_op jit(solution)/shard_map/ppermute | solution.py:26
  57.6 20.5 %copy-start.4 = (bf16[768,768]{1,0:T(8,128)(2,1)}, bf16[768,768]{1,0:T(8,128)(2,1)S(1)}, u32[]{:S(2)}) copy-start(bf16[768,768]{1,0:T(8,128)(2,1)S(1)} %collective-permute-done.9.refs_3_) | copy-start | bytes 3538948
  57.6 20.5 %collective-permute-start.13 = (bf16[768,768]{1,0:T(8,128)(2,1)S(1)}, bf16[768,768]{1,0:T(8,128)(2,1)}, u32[]{:S(2)}, u32[]{:S(2)}) collective-permute-start(bf16[768,768]{1,0:T(8,128)(2,1)S(1)} %collective-permute-done.9.refs_3_), channel_id=1, source_target_pairs={{0,4},{4,0},{8,12},{12,8},{16,20},{20,16},{24,28},{28,24},{1,5},{5... | collective-permute-start | bytes 3538952 | tf_op jit(solution)/shard_map/ppermute | solution.py:26
  57.7 26.7 %collective-permute-start.18 = (bf16[256,1536]{1,0:T(8,128)(2,1)}, bf16[256,1536]{1,0:T(8,128)(2,1)}, u32[]{:S(2)}, u32[]{:S(2)}) collective-permute-start(bf16[256,1536]{1,0:T(8,128)(2,1)} %collective-permute-done.15.refs_10_), channel_id=1, source_target_pairs={{2,3},{6,7},{10,11},{14,15},{18,19},{22,23},{26,27},{30,31}} | collective-permute-start | bytes 2359304 | tf_op jit(solution)/shard_map/ppermute | solution.py:26
  74.9 17.8 %collective-permute-start.19 = (bf16[256,1536]{1,0:T(8,128)(2,1)}, bf16[256,1536]{1,0:T(8,128)(2,1)}, u32[]{:S(2)}, u32[]{:S(2)}) collective-permute-start(bf16[256,1536]{1,0:T(8,128)(2,1)} %collective-permute-done.17.refs_12_), channel_id=1, source_target_pairs={{1,0},{5,4},{9,8},{13,12},{17,16},{21,20},{25,24},{29,28}} | collective-permute-start | bytes 2359304 | tf_op jit(solution)/shard_map/ppermute | solution.py:26
  76.2 22.3 %collective-permute-start = (bf16[128,1536]{1,0:T(8,128)(2,1)}, bf16[128,1536]{1,0:T(8,128)(2,1)}, u32[]{:S(2)}, u32[]{:S(2)}) collective-permute-start(bf16[128,1536]{1,0:T(8,128)(2,1)} %refs_0_.1), channel_id=1, source_target_pairs={{0,8},{4,20},{8,0},{12,28},{16,24},{20,4},{24,16},{28,12},{1,9},{5... | collective-permute-start | bytes 1179656 | tf_op jit(solution)/shard_map/ppermute | solution.py:26
  76.3 31.5 %collective-permute-start.1 = (bf16[128,1536]{1,0:T(8,128)(2,1)}, bf16[128,1536]{1,0:T(8,128)(2,1)}, u32[]{:S(2)}, u32[]{:S(2)}) collective-permute-start(bf16[128,1536]{1,0:T(8,128)(2,1)} %refs_0_.1), channel_id=1, source_target_pairs={{0,16},{4,12},{8,24},{12,4},{16,0},{20,28},{24,8},{28,20},{1,17},{... | collective-permute-start | bytes 1179656 | tf_op jit(solution)/shard_map/ppermute | solution.py:26
  96.4 9.5 %collective-permute-start.20 = (bf16[256,512]{1,0:T(8,128)(2,1)}, bf16[256,512]{1,0:T(8,128)(2,1)S(1)}, u32[]{:S(2)}, u32[]{:S(2)}) collective-permute-start(bf16[256,512]{1,0:T(8,128)(2,1)} %get-tuple-element.8.refs_0_), channel_id=1, source_target_pairs={{0,8},{4,20},{8,0},{12,28},{16,24},{20,4},{24,16},{28,12},{1,9},{5... | collective-permute-start | bytes 786440 | tf_op jit(solution)/shard_map/ppermute | solution.py:26
  96.5 11.3 %collective-permute-start.21 = (bf16[256,512]{1,0:T(8,128)(2,1)}, bf16[256,512]{1,0:T(8,128)(2,1)S(1)}, u32[]{:S(2)}, u32[]{:S(2)}) collective-permute-start(bf16[256,512]{1,0:T(8,128)(2,1)} %get-tuple-element.8.refs_0_), channel_id=1, source_target_pairs={{0,16},{4,12},{8,24},{12,4},{16,0},{20,28},{24,8},{28,20},{1,17},{... | collective-permute-start | bytes 786440 | tf_op jit(solution)/shard_map/ppermute | solution.py:26
  98.5 9.8 %collective-permute-start.2 = (bf16[128,1536]{1,0:T(8,128)(2,1)}, bf16[128,1536]{1,0:T(8,128)(2,1)S(1)}, u32[]{:S(2)}, u32[]{:S(2)}) collective-permute-start(bf16[128,1536]{1,0:T(8,128)(2,1)} %collective-permute-done.refs_1_), channel_id=1, source_target_pairs={{0,16},{4,12},{8,24},{12,4},{16,0},{20,28},{24,8},{28,20},{1,17},{... | collective-permute-start | bytes 1179656 | tf_op jit(solution)/shard_map/ppermute | solution.py:26
  98.6 9.8 %collective-permute-start.23 = (bf16[256,512]{1,0:T(8,128)(2,1)}, bf16[256,512]{1,0:T(8,128)(2,1)S(1)}, u32[]{:S(2)}, u32[]{:S(2)}) collective-permute-start(bf16[256,512]{1,0:T(8,128)(2,1)} %get-tuple-element.8.refs_0_), channel_id=1, source_target_pairs={{0,4},{4,0},{8,12},{12,8},{16,20},{20,16},{24,28},{28,24},{1,5},{5... | collective-permute-start | bytes 786440 | tf_op jit(solution)/shard_map/ppermute | solution.py:26
  105.8 8.6 %copy-start.16 = (bf16[256,512]{1,0:T(8,128)(2,1)}, bf16[256,512]{1,0:T(8,128)(2,1)S(1)}, u32[]{:S(2)}) copy-start(bf16[256,512]{1,0:T(8,128)(2,1)S(1)} %collective-permute-done.20.refs_1_) | copy-start | bytes 786436
  105.9 6.4 %collective-permute-start.22 = (bf16[256,512]{1,0:T(8,128)(2,1)S(1)}, bf16[256,512]{1,0:T(8,128)(2,1)S(1)}, u32[]{:S(2)}, u32[]{:S(2)}) collective-permute-start(bf16[256,512]{1,0:T(8,128)(2,1)S(1)} %collective-permute-done.20.refs_1_), channel_id=1, source_target_pairs={{0,16},{4,12},{8,24},{12,4},{16,0},{20,28},{24,8},{28,20},{1,17},{... | collective-permute-start | bytes 786440 | tf_op jit(solution)/shard_map/ppermute | solution.py:26
  107.8 4.4 %collective-permute-start.24 = (bf16[256,512]{1,0:T(8,128)(2,1)S(1)}, bf16[256,512]{1,0:T(8,128)(2,1)S(1)}, u32[]{:S(2)}, u32[]{:S(2)}) collective-permute-start(bf16[256,512]{1,0:T(8,128)(2,1)S(1)} %collective-permute-done.20.refs_1_), channel_id=1, source_target_pairs={{0,4},{4,0},{8,12},{12,8},{16,20},{20,16},{24,28},{28,24},{1,5},{5... | collective-permute-start | bytes 786440 | tf_op jit(solution)/shard_map/ppermute | solution.py:26
  107.8 6.7 %copy-start.17 = (bf16[256,512]{1,0:T(8,128)(2,1)}, bf16[256,512]{1,0:T(8,128)(2,1)S(1)}, u32[]{:S(2)}) copy-start(bf16[256,512]{1,0:T(8,128)(2,1)S(1)} %collective-permute-done.21.refs_2_) | copy-start | bytes 786436
  107.8 4.9 %collective-permute-start.25 = (bf16[256,512]{1,0:T(8,128)(2,1)S(1)}, bf16[256,512]{1,0:T(8,128)(2,1)S(1)}, u32[]{:S(2)}, u32[]{:S(2)}) collective-permute-start(bf16[256,512]{1,0:T(8,128)(2,1)S(1)} %collective-permute-done.21.refs_2_), channel_id=1, source_target_pairs={{0,4},{4,0},{8,12},{12,8},{16,20},{20,16},{24,28},{28,24},{1,5},{5... | collective-permute-start | bytes 786440 | tf_op jit(solution)/shard_map/ppermute | solution.py:26
  108.3 11.2 %copy-start.10 = (bf16[128,1536]{1,0:T(8,128)(2,1)}, bf16[128,1536]{1,0:T(8,128)(2,1)S(1)}, u32[]{:S(2)}) copy-start(bf16[128,1536]{1,0:T(8,128)(2,1)S(1)} %collective-permute-done.2.refs_3_) | copy-start | bytes 1179652
  108.3 11.2 %collective-permute-start.3 = (bf16[128,1536]{1,0:T(8,128)(2,1)}, bf16[128,1536]{1,0:T(8,128)(2,1)S(1)}, u32[]{:S(2)}, u32[]{:S(2)}) collective-permute-start(bf16[128,1536]{1,0:T(8,128)(2,1)} %refs_0_.1), channel_id=1, source_target_pairs={{0,4},{4,0},{8,12},{12,8},{16,20},{20,16},{24,28},{28,24},{1,5},{5... | collective-permute-start | bytes 1179656 | tf_op jit(solution)/shard_map/ppermute | solution.py:26
  108.4 6.1 %copy-start.18 = (bf16[256,512]{1,0:T(8,128)(2,1)}, bf16[256,512]{1,0:T(8,128)(2,1)S(1)}, u32[]{:S(2)}) copy-start(bf16[256,512]{1,0:T(8,128)(2,1)S(1)} %collective-permute-done.23.refs_4_) | copy-start | bytes 786436
  108.4 11.3 %collective-permute-start.4 = (bf16[128,1536]{1,0:T(8,128)(2,1)}, bf16[128,1536]{1,0:T(8,128)(2,1)S(1)}, u32[]{:S(2)}, u32[]{:S(2)}) collective-permute-start(bf16[128,1536]{1,0:T(8,128)(2,1)} %collective-permute-done.refs_1_), channel_id=1, source_target_pairs={{0,4},{4,0},{8,12},{12,8},{16,20},{20,16},{24,28},{28,24},{1,5},{5... | collective-permute-start | bytes 1179656 | tf_op jit(solution)/shard_map/ppermute | solution.py:26
  112.2 2.3 %copy-start.19 = (bf16[256,512]{1,0:T(8,128)(2,1)}, bf16[256,512]{1,0:T(8,128)(2,1)S(1)}, u32[]{:S(2)}) copy-start(bf16[256,512]{1,0:T(8,128)(2,1)S(1)} %collective-permute-done.22.refs_3_) | copy-start | bytes 786436
  112.2 1.5 %collective-permute-start.26 = (bf16[256,512]{1,0:T(8,128)(2,1)S(1)}, bf16[256,512]{1,0:T(8,128)(2,1)S(1)}, u32[]{:S(2)}, u32[]{:S(2)}) collective-permute-start(bf16[256,512]{1,0:T(8,128)(2,1)S(1)} %collective-permute-done.22.refs_3_), channel_id=1, source_target_pairs={{0,4},{4,0},{8,12},{12,8},{16,20},{20,16},{24,28},{28,24},{1,5},{5... | collective-permute-start | bytes 786440 | tf_op jit(solution)/shard_map/ppermute | solution.py:26
  112.2 11.2 %collective-permute-start.5 = (bf16[128,1536]{1,0:T(8,128)(2,1)}, bf16[128,1536]{1,0:T(8,128)(2,1)S(1)}, u32[]{:S(2)}, u32[]{:S(2)}) collective-permute-start(bf16[128,1536]{1,0:T(8,128)(2,1)} %collective-permute-done.1.refs_2_), channel_id=1, source_target_pairs={{0,4},{4,0},{8,12},{12,8},{16,20},{20,16},{24,28},{28,24},{1,5},{5... | collective-permute-start | bytes 1179656 | tf_op jit(solution)/shard_map/ppermute | solution.py:26
  112.7 10.7 %collective-permute-start.6 = (bf16[128,1536]{1,0:T(8,128)(2,1)S(1)}, bf16[128,1536]{1,0:T(8,128)(2,1)S(1)}, u32[]{:S(2)}, u32[]{:S(2)}) collective-permute-start(bf16[128,1536]{1,0:T(8,128)(2,1)S(1)} %collective-permute-done.2.refs_3_), channel_id=1, source_target_pairs={{0,4},{4,0},{8,12},{12,8},{16,20},{20,16},{24,28},{28,24},{1,5},{5... | collective-permute-start | bytes 1179656 | tf_op jit(solution)/shard_map/ppermute | solution.py:26
  119.5 7.8 %collective-permute-start.27 = (bf16[256,256]{1,0:T(8,128)(2,1)}, bf16[256,256]{1,0:T(8,128)(2,1)S(1)}, u32[]{:S(2)}, u32[]{:S(2)}) collective-permute-start(bf16[256,256]{1,0:T(8,128)(2,1)} %shard_map.66.refs_8_), channel_id=1, source_target_pairs={{0,1},{1,2},{2,3},{3,0},{4,5},{5,6},{6,7},{7,4},{8,9},{9,10},{10,1... | collective-permute-start | bytes 393224 | tf_op jit(solution)/shard_map/ppermute | solution.py:26
  119.6 12.4 %copy-start.11 = (bf16[128,1536]{1,0:T(8,128)(2,1)}, bf16[128,1536]{1,0:T(8,128)(2,1)S(1)}, u32[]{:S(2)}) copy-start(bf16[128,1536]{1,0:T(8,128)(2,1)S(1)} %collective-permute-done.3.refs_4_) | copy-start | bytes 1179652
  119.6 12.4 %collective-permute-start.28 = (bf16[256,256]{1,0:T(8,128)(2,1)}, bf16[256,256]{1,0:T(8,128)(2,1)S(1)}, u32[]{:S(2)}, u32[]{:S(2)}) collective-permute-start(bf16[256,256]{1,0:T(8,128)(2,1)} %shard_map.66.refs_8_), channel_id=1, source_target_pairs={{0,2},{1,3},{2,0},{3,1},{4,6},{5,7},{6,4},{7,5},{8,10},{9,11},{10,... | collective-permute-start | bytes 393224 | tf_op jit(solution)/shard_map/ppermute | solution.py:26
  119.8 12.2 %copy-start.12 = (bf16[128,1536]{1,0:T(8,128)(2,1)}, bf16[128,1536]{1,0:T(8,128)(2,1)S(1)}, u32[]{:S(2)}) copy-start(bf16[128,1536]{1,0:T(8,128)(2,1)S(1)} %collective-permute-done.4.refs_5_) | copy-start | bytes 1179652
  119.8 12.2 %collective-permute-start.29 = (bf16[256,256]{1,0:T(8,128)(2,1)}, bf16[256,256]{1,0:T(8,128)(2,1)S(1)}, u32[]{:S(2)}, u32[]{:S(2)}) collective-permute-start(bf16[256,256]{1,0:T(8,128)(2,1)} %shard_map.66.refs_8_), channel_id=1, source_target_pairs={{0,3},{1,0},{2,1},{3,2},{4,7},{5,4},{6,5},{7,6},{8,11},{9,8},{10,9... | collective-permute-start | bytes 393224 | tf_op jit(solution)/shard_map/ppermute | solution.py:26
  123.5 8.5 %copy-start.13 = (bf16[128,1536]{1,0:T(8,128)(2,1)}, bf16[128,1536]{1,0:T(8,128)(2,1)S(1)}, u32[]{:S(2)}) copy-start(bf16[128,1536]{1,0:T(8,128)(2,1)S(1)} %collective-permute-done.5.refs_6_) | copy-start | bytes 1179652
  123.5 8.5 %copy-start.14 = (bf16[128,1536]{1,0:T(8,128)(2,1)}, bf16[128,1536]{1,0:T(8,128)(2,1)S(1)}, u32[]{:S(2)}) copy-start(bf16[128,1536]{1,0:T(8,128)(2,1)S(1)} %collective-permute-done.6.refs_7_) | copy-start | bytes 1179652
  127.3 4.7 %copy-start.23 = (bf16[256,256]{1,0:T(8,128)(2,1)}, bf16[256,256]{1,0:T(8,128)(2,1)S(1)}, u32[]{:S(2)}) copy-start(bf16[256,256]{1,0:T(8,128)(2,1)S(1)} %collective-permute-done.27.refs_9_) | copy-start | bytes 393220
  (8 other events, 12.0 us)
where the time goes:
time: 139 us; the launch traced here: 137 us
  waiting for transfers between devices  84.9 us (61%)
  starting transfers between devices  28.9 us (21%)
  Pallas kernels  18.8 us (14%)
  local copies, waits for them, and re-layouts  4.24 us (3%)
    ppermute x30, waiting for transfers between devices, permute(): return lax.ppermute(x, axes, pairs)  84.9 us
    ppermute x30, starting transfers between devices, permute(): return lax.ppermute(x, axes, pairs)  28.9 us
    pallas_call x4, Pallas kernels, call(): return pl.pallas_call(kernel, cost_estimate=cost, **settings)(*args)  18.8 us
    unnamed x54, local copies, waits for them, and re-layouts  4.21 us
  transfers between devices with their start and end apart: 30, of which 10 were waited for; matrix products, arithmetic and copies ran while one was open for 0% of the time, Pallas kernels for 11%

commit v1 on v0

--- a/solution.py
+++ b/solution.py
@@ -7,6 +7,7 @@
 
 HS = 128
 NEG = -1e30
+SPARE = 4 << 20
 BF16 = jnp.bfloat16
 F32 = jnp.float32
 ANY = pl.BlockSpec(memory_space=pl.ANY)
@@ -45,14 +46,22 @@
     return [permute(piece, "seq", pairs) for piece in pieces]
 
 
+def line_sources(step, chain, at):
+    return (at + step + chain) % 2 == 0
+
+
 def line_gather(x, count):
-    below, above = [x], [x]
+    chains = [[x], [x]]
     for k in range(1, count):
-        up = [(i, i + 1) for i in range(k - 1, count - 1)]
-        down = [(i + 1, i) for i in range(count - k)]
-        below.append(permute(below[-1], "tensor", up))
-        above.append(permute(above[-1], "tensor", down))
-    return below, above
+        for chain in (1, 0):
+            pairs = []
+            for i in range(count):
+                up = line_sources(k, chain, i)
+                if 0 <= (i - k if up else i + k) < count:
+                    pairs.append((i - 1 if up else i + 1, i))
+            if pairs:
+                chains[chain].append(permute(chains[chain][-1], "tensor", pairs))
+    return chains
 
 
 def place():
@@ -83,14 +92,12 @@
 
         x_copy(at, xs[0]).start()
         for k in range(1, steps + 1):
-
-            @pl.when(at >= k)
-            def _():
-                x_copy(at - k, xs[k]).start()
-
-            @pl.when(at + k < count)
-            def _():
-                x_copy(at + k, xs[steps + k]).start()
+            for chain in range(2):
+                block = jnp.where(line_sources(k, chain, at), at - k, at + k)
+
+                @pl.when((block >= 0) & (block < count))
+                def _():
+                    x_copy(block, xs[chain * steps + k]).start()
 
         acc[...] = jnp.zeros(acc.shape, F32)
         depth = x_full.shape[2]
@@ -118,8 +125,8 @@
 
     def kernel(*refs):
         mine, theirs = refs[:chips], refs[chips : 2 * chips]
-        acc_in, from_below, from_above, q_out, kv_out = refs[2 * chips : 2 * chips + 5]
-        acc, x_block, w_block, w_sem, x_sem, acc_sem = refs[2 * chips + 5 :]
+        acc_in, x_in, q_out, kv_out = refs[2 * chips : 2 * chips + 4]
+        acc, x_block, w_block, w_sem, x_sem, acc_sem = refs[2 * chips + 4 :]
         chip, core, at = place()
         rows = mine[0].shape[0]
         get_acc = pltpu.make_async_copy(acc_in, acc, acc_sem)
@@ -129,16 +136,11 @@
         def w_copy(kind, source):
             return pltpu.make_async_copy(source, w_block.at[pl.ds(pl.multiple_of(kind * rows, rows), rows)], w_sem.at[kind])
 
-        def x_copy(source):
-            return pltpu.make_async_copy(source, x_block, x_sem)
-
-        @pl.when(at == 0)
+        x_copy = pltpu.make_async_copy(x_in, x_block, x_sem)
+
+        @pl.when(edge)
         def _():
-            x_copy(from_above).start()
-
-        @pl.when(at == count - 1)
-        def _():
-            x_copy(from_below).start()
+            x_copy.start()
 
         wanted = jnp.where(at == 0, count - 1, 0)
         for p in range(chips):
@@ -155,7 +157,7 @@
 
         @pl.when(edge)
         def _():
-            x_copy(from_below).wait()
+            x_copy.wait()
             w_copy(0, mine[0]).wait()
             w_copy(1, mine[0]).wait()
             acc[...] += jnp.dot(x_block[...], w_block[...], preferred_element_type=F32)
@@ -172,7 +174,7 @@
 
     def kernel(ids, key_ids, q_ref, *refs):
         mine, theirs = refs[:chips], refs[chips : 2 * chips]
-        out_ref, kv, sem = refs[2 * chips :]
+        out_ref, kv, scores, sem = refs[2 * chips :]
         chip, core, _ = place()
         copies = []
         for p in range(chips):
@@ -198,27 +200,42 @@
         for copy in copies:
             copy.wait()
 
-        def step(block, carry):
+        lanes = [slice(i * HS, (i + 1) * HS) for i in range(rows // HS)]
+
+        def score(block, tops):
             here = kv[block]
             same = row_ids == key_ids[block]
             result = []
-            for h, (top, total, out) in enumerate(carry):
+            for h, top in enumerate(tops):
                 keys = here[:, h * HS : (h + 1) * HS]
+                dots = lax.dot_general(
+                    queries[h], keys, (((1,), (1,)), ((), ())), preferred_element_type=F32
+                )
+                dots = jnp.where(same, dots, NEG)
+                scores[h, block] = dots
+                for lane in lanes:
+                    top = jnp.maximum(top, dots[:, lane])
+                result.append(top)
+            return tuple(result)
+
+        tops = lax.fori_loop(low, high, score, (jnp.full((rows, HS), NEG, F32),) * 2)
+        tops = [jnp.max(top, axis=1, keepdims=True) for top in tops]
+
+        def weigh(block, carry):
+            here = kv[block]
+            result = []
+            for h, (total, out) in enumerate(carry):
                 values = here[:, width + h * HS : width + (h + 1) * HS]
-                scores = lax.dot_general(
-                    queries[h], keys, (((1,), (1,)), ((), ())), preferred_element_type=F32
-                ) * (HS**-0.5)
-                scores = jnp.where(same, scores, NEG)
-                new_top = jnp.maximum(top, jnp.max(scores, axis=1, keepdims=True))
-                probs = jnp.exp(scores - new_top)
-                fade = jnp.exp(top - new_top)
-                total = total * fade + jnp.sum(probs, axis=1, keepdims=True)
-                out = out * fade + jnp.dot(probs.astype(BF16), values, preferred_element_type=F32)
-                result.append((new_top, total, out))
+                probs = jnp.exp((scores[h, block] - tops[h]) * (HS**-0.5))
+                for lane in lanes:
+                    total = total + probs[:, lane]
+                out = out + jnp.dot(probs.astype(BF16), values, preferred_element_type=F32)
+                result.append((total, out))
             return tuple(result)
 
-        start = (jnp.full((rows, 1), NEG, F32), jnp.zeros((rows, 1), F32), jnp.zeros((rows, HS), F32))
-        for h, (_, total, out) in enumerate(lax.fori_loop(low, high, step, (start, start))):
+        zero = jnp.zeros((rows, HS), F32)
+        for h, (total, out) in enumerate(lax.fori_loop(low, high, weigh, ((zero, zero),) * 2)):
+            total = jnp.sum(total, axis=1, keepdims=True)
             out_ref[:, h * HS : (h + 1) * HS] = (out / total).astype(BF16)
 
     return kernel
@@ -256,9 +273,10 @@
     return kernel
 
 
-def call(kernel, *args, flops, read, exps=0, **settings):
+def call(kernel, *args, flops, read, vmem, exps=0, **settings):
     cost = pl.CostEstimate(flops=flops, bytes_accessed=read, transcendentals=exps)
-    return pl.pallas_call(kernel, cost_estimate=cost, **settings)(*args)
+    limit = pltpu.CompilerParams(vmem_limit_bytes=vmem)
+    return pl.pallas_call(kernel, cost_estimate=cost, compiler_params=limit, **settings)(*args)
 
 
 def steps_on_device(patches, segment_ids, w_query, w_key, w_value, w_out):
@@ -272,7 +290,7 @@
     cols = 3 * width
     steps = count - 2
 
-    below, above = line_gather(patches, count)
+    chain0, chain1 = line_gather(patches, count)
     w_mine = gather_chips(jnp.concatenate([w_query, w_key, w_value], axis=1), chips)
     w_theirs = swap_cores(w_mine, devices)
     out_mine = gather_chips(w_out, chips)
@@ -282,10 +300,11 @@
         project_most(chips, count, steps),
         *w_mine,
         *w_theirs,
-        *below[: steps + 1],
-        *above[1 : steps + 1],
+        *chain0[: steps + 1],
+        *chain1[1 : steps + 1],
         flops=2 * rows * cols * depth * count,
         read=2 * count * depth * (rows + cols),
+        vmem=2 * count * depth * (rows + cols) + 8 * rows * cols + SPARE,
         out_shape=shape((rows, cols), F32),
         in_specs=[ANY] * (2 * chips + 1 + 2 * steps),
         out_specs=VMEM,
@@ -301,12 +320,12 @@
         *w_mine,
         *w_theirs,
         acc,
-        below[-1],
-        above[-1],
+        chain0[-1],
         flops=2 * rows * cols * depth,
         read=2 * depth * (rows + cols) + 4 * rows * cols,
+        vmem=2 * depth * (rows + cols) + 8 * rows * cols + SPARE,
         out_shape=[shape((rows, width), BF16), shape((rows, 2 * width), BF16)],
-        in_specs=[ANY] * (2 * chips + 3),
+        in_specs=[ANY] * (2 * chips + 2),
         out_specs=[VMEM] * 2,
         scratch_shapes=[
             pltpu.VMEM((rows, cols), F32),
@@ -333,7 +352,12 @@
         out_shape=shape((rows, width), BF16),
         in_specs=[SMEM, VMEM, VMEM] + [ANY] * (2 * chips),
         out_specs=VMEM,
-        scratch_shapes=[pltpu.VMEM((devices, rows, 2 * width), BF16), dma((devices,))],
+        scratch_shapes=[
+            pltpu.VMEM((devices, rows, 2 * width), BF16),
+            pltpu.VMEM((2, devices, rows, rows), F32),
+            dma((devices,)),
+        ],
+        vmem=devices * rows * (4 * width + 8 * rows) + SPARE,
     )
 
     all_heads = [heads]
@@ -346,6 +370,7 @@
         *all_heads,
         flops=2 * rows * devices * HS * w_out.shape[1],
         read=2 * devices * HS * (rows + w_out.shape[1]),
+        vmem=2 * devices * HS * (rows + w_out.shape[1]) + 8 * rows * w_out.shape[1] + SPARE,
         out_shape=shape((rows, w_out.shape[1]), BF16),
         in_specs=[ANY] * (2 * chips + count),
         out_specs=VMEM,

time: 139 us -> 135 us (0.971)
  waiting for transfers between devices: 84.9 us -> 91.7 us
  Pallas kernels: 18.8 us -> 12.4 us
  starting transfers between devices: 28.9 us -> 26.6 us
  local copies, waits for them, and re-layouts: 4.24 us -> 2.21 us
    ppermute x30 -> x29, waiting for transfers between devices: 84.9 us -> 91.7 us  [permute(): return lax.ppermute(x, axes, pairs)]
    pallas_call x4, Pallas kernels: 18.8 us -> 12.4 us  [call(): pl.pallas_call(kernel, cost_estimate=cost, compiler_params=limit, **setti...]
    ppermute x30 -> x29, starting transfers between devices: 28.9 us -> 26.6 us  [permute(): return lax.ppermute(x, axes, pairs)]
    unnamed x54 -> x10, local copies, waits for them, and re-layouts: 4.21 us -> 2.18 us
  transfers between devices with their start and end apart: 30 -> 29, of which waited for: 10 -> 10; matrix products, arithmetic and copies ran while one was open for 0% -> 0% of each run, Pallas kernels for 11% -> 7%
where the time goes in v1:
time: 135 us; the launch traced here: 133 us
  waiting for transfers between devices  91.7 us (68%)
  starting transfers between devices  26.6 us (20%)
  Pallas kernels  12.4 us (9%)
  local copies, waits for them, and re-layouts  2.21 us (2%)
    ppermute x29, waiting for transfers between devices, permute(): return lax.ppermute(x, axes, pairs)  91.7 us
    ppermute x29, starting transfers between devices, permute(): return lax.ppermute(x, axes, pairs)  26.6 us
    pallas_call x4, Pallas kernels, call(): pl.pallas_call(kernel, cost_estimate=cost, compiler_params=limit, **setti...  12.4 us
  transfers between devices with their start and end apart: 29, of which 10 were waited for; matrix products, arithmetic and copies ran while one was open for 0% of the time, Pallas kernels for 7%

profile of v1, /device:TPU:0, one launch (start us, length us, event | category | flops | bytes accessed | tf_op | source)
XLA Modules:
  0.0 133.0 jit_solution(1269517043189259714)
XLA Ops:
  0.0 1.1 constant_dynamic-update-slice_fusion.2
  1.1 1.0 constant_dynamic-update-slice_fusion.1
  2.2 3.0 %collective-permute-start.7 = (bf16[768,768]{1,0:T(8,128)(2,1)S(1)}, bf16[768,768]{1,0:T(8,128)(2,1)S(1)}, u32[]{:S(2)}, u32[]{:S(2)}) collective-permute-start(bf16[768,768]{1,0:T(8,128)(2,1)S(1)} %constant_dynamic-update-slice_fusion.refs_0_), channel_id=1, source_target_pairs={{0,8},{4,20},{8,0},{12,28},{16,24},{20,4},{24,16},{28,12},{1,9},{5... | collective-permute-start | bytes 3538952 | tf_op jit(solution)/shard_map/ppermute | solution.py:27
  5.3 1.5 %collective-permute-start.8 = (bf16[768,768]{1,0:T(8,128)(2,1)S(1)}, bf16[768,768]{1,0:T(8,128)(2,1)S(1)}, u32[]{:S(2)}, u32[]{:S(2)}) collective-permute-start(bf16[768,768]{1,0:T(8,128)(2,1)S(1)} %constant_dynamic-update-slice_fusion.refs_0_), channel_id=1, source_target_pairs={{0,16},{4,12},{8,24},{12,4},{16,0},{20,28},{24,8},{28,20},{1,17},{... | collective-permute-start | bytes 3538952 | tf_op jit(solution)/shard_map/ppermute | solution.py:27
  6.8 24.7 %collective-permute-done.7.refs_1_ = bf16[768,768]{1,0:T(8,128)(2,1)S(1)} collective-permute-done((bf16[768,768]{1,0:T(8,128)(2,1)S(1)}, bf16[768,768]{1,0:T(8,128)(2,1)S(1)}, u32[]{:S(2)}, u32[]{:S(2)}) %collective-permute-start.7) | collective-permute-done | bytes 1179680 | tf_op jit(solution)/shard_map/ppermute | solution.py:27
  31.5 1.6 %collective-permute-start.9 = (bf16[768,768]{1,0:T(8,128)(2,1)S(1)}, bf16[768,768]{1,0:T(8,128)(2,1)S(1)}, u32[]{:S(2)}, u32[]{:S(2)}) collective-permute-start(bf16[768,768]{1,0:T(8,128)(2,1)S(1)} %collective-permute-done.7.refs_1_), channel_id=1, source_target_pairs={{0,16},{4,12},{8,24},{12,4},{16,0},{20,28},{24,8},{28,20},{1,17},{... | collective-permute-start | bytes 3538952 | tf_op jit(solution)/shard_map/ppermute | solution.py:27
  33.1 1.7 %collective-permute-start.14 = (bf16[256,1536]{1,0:T(8,128)(2,1)S(1)}, bf16[256,1536]{1,0:T(8,128)(2,1)S(1)}, u32[]{:S(2)}, u32[]{:S(2)}) collective-permute-start(bf16[256,1536]{1,0:T(8,128)(2,1)S(1)} %copy-done), channel_id=1, source_target_pairs={{1,0},{0,1},{3,2},{2,3},{5,4},{4,5},{7,6},{6,7},{9,8},{8,9},{11,10... | collective-permute-start | bytes 2359304 | tf_op jit(solution)/shard_map/ppermute | solution.py:27
  34.8 0.0 collective-permute-start.10
  34.8 0.7 collective-permute-start.16
  35.5 15.5 %collective-permute-done.14.refs_9_ = bf16[256,1536]{1,0:T(8,128)(2,1)S(1)} collective-permute-done((bf16[256,1536]{1,0:T(8,128)(2,1)S(1)}, bf16[256,1536]{1,0:T(8,128)(2,1)S(1)}, u32[]{:S(2)}, u32[]{:S(2)}) %collective-permute-start.14) | collective-permute-done | bytes 786464 | tf_op jit(solution)/shard_map/ppermute | solution.py:27
  51.0 0.7 collective-permute-start.15
  51.8 0.1 collective-permute-start.11
  51.8 0.0 collective-permute-done.8.refs_2_
  51.8 0.5 collective-permute-start.12
  52.3 0.0 collective-permute-done.9.refs_3_
  52.3 0.1 collective-permute-start.13
  52.4 1.3 collective-permute-start.17
  53.7 0.0 collective-permute-done.15.refs_10_
  53.7 1.3 collective-permute-start.18
  55.0 23.5 %collective-permute-done.17.refs_12_ = bf16[256,1536]{1,0:T(8,128)(2,1)S(1)} collective-permute-done((bf16[256,1536]{1,0:T(8,128)(2,1)S(1)}, bf16[256,1536]{1,0:T(8,128)(2,1)S(1)}, u32[]{:S(2)}, u32[]{:S(2)}) %collective-permute-start.17) | collective-permute-done | bytes 786464 | tf_op jit(solution)/shard_map/ppermute | solution.py:27
  78.5 1.5 %collective-permute-start = (bf16[128,1536]{1,0:T(8,128)(2,1)S(1)}, bf16[128,1536]{1,0:T(8,128)(2,1)S(1)}, u32[]{:S(2)}, u32[]{:S(2)}) collective-permute-start(bf16[128,1536]{1,0:T(8,128)(2,1)S(1)} %copy-done.1), channel_id=1, source_target_pairs={{0,8},{4,20},{8,0},{12,28},{16,24},{20,4},{24,16},{28,12},{1,9},{5... | collective-permute-start | bytes 1179656 | tf_op jit(solution)/shard_map/ppermute | solution.py:27
  80.0 0.0 collective-permute-done.11.refs_5_
  80.0 1.3 collective-permute-start.1
  81.3 4.7 %shard_map.64.refs_8_ = f32[256,768]{1,0:T(8,128)S(1)} custom-call(bf16[768,768]{1,0:T(8,128)(2,1)S(1)} %constant_dynamic-update-slice_fusion.refs_0_, bf16[768,768]{1,0:T(8,128)(2,1)S(1)} %collective-permute-done.7.refs_1_, bf16[768,768]{1,0:T(8,128)(2,1)S(1)} %collective-permute-done.8.refs_2_, bf16[768,768]{1,0:T(8,128)(2,1)S(1)} %collective-permute-done.9.refs_3_, ...), custom_call_target="tpu_custom_call" | custom-call | flops 2415919104 | bytes 12582912 | tf_op jit(solution)/shard_map/pallas_call | solution.py:279
  86.0 0.0 copy-start.2
  86.0 9.1 %collective-permute-done.18.refs_9_ = bf16[256,1536]{1,0:T(8,128)(2,1)S(1)} collective-permute-done((bf16[256,1536]{1,0:T(8,128)(2,1)S(1)}, bf16[256,1536]{1,0:T(8,128)(2,1)S(1)}, u32[]{:S(2)}, u32[]{:S(2)}) %collective-permute-start.18) | collective-permute-done | bytes 786464 | tf_op jit(solution)/shard_map/ppermute | solution.py:27
  95.1 1.5 %shard_map.65 = (bf16[256,256]{1,0:T(8,128)(2,1)S(1)}, bf16[256,512]{1,0:T(8,128)(2,1)S(1)}) custom-call(bf16[768,768]{1,0:T(8,128)(2,1)S(1)} %constant_dynamic-update-slice_fusion.refs_0_, bf16[768,768]{1,0:T(8,128)(2,1)S(1)} %collective-permute-done.7.refs_1_, bf16[768,768]{1,0:T(8,128)(2,1)S(1)} %collective-permute-done.8.refs_2_, ...), custom_call_target="tpu_custom_call" | custom-call | flops 603979776 | bytes 3932160 | tf_op jit(solution)/shard_map/pallas_call | solution.py:279
  96.6 1.6 %collective-permute-start.19 = (bf16[256,512]{1,0:T(8,128)(2,1)S(1)}, bf16[256,512]{1,0:T(8,128)(2,1)S(1)}, u32[]{:S(2)}, u32[]{:S(2)}) collective-permute-start(bf16[256,512]{1,0:T(8,128)(2,1)S(1)} %get-tuple-element.8.refs_0_), channel_id=1, source_target_pairs={{0,8},{4,20},{8,0},{12,28},{16,24},{20,4},{24,16},{28,12},{1,9},{5... | collective-permute-start | bytes 786440 | tf_op jit(solution)/shard_map/ppermute | solution.py:27
  98.1 1.3 collective-permute-start.20
  99.5 0.7 collective-permute-start.2
  100.2 5.7 %collective-permute-done.19.refs_1_ = bf16[256,512]{1,0:T(8,128)(2,1)S(1)} collective-permute-done((bf16[256,512]{1,0:T(8,128)(2,1)S(1)}, bf16[256,512]{1,0:T(8,128)(2,1)S(1)}, u32[]{:S(2)}, u32[]{:S(2)}) %collective-permute-start.19) | collective-permute-done | bytes 262176 | tf_op jit(solution)/shard_map/ppermute | solution.py:27
  105.8 1.3 collective-permute-start.21
  107.1 0.5 collective-permute-start.24
  107.7 1.3 collective-permute-done.2.refs_3_
  108.9 1.1 collective-permute-start.3
  110.1 0.0 collective-permute-start.4
  110.1 2.1 %collective-permute-done.21.refs_3_ = bf16[256,512]{1,0:T(8,128)(2,1)S(1)} collective-permute-done((bf16[256,512]{1,0:T(8,128)(2,1)S(1)}, bf16[256,512]{1,0:T(8,128)(2,1)S(1)}, u32[]{:S(2)}, u32[]{:S(2)}) %collective-permute-start.21) | collective-permute-done | bytes 262176 | tf_op jit(solution)/shard_map/ppermute | solution.py:27
  112.2 0.4 collective-permute-start.25
  112.6 0.1 collective-permute-start.5
  112.7 0.4 collective-permute-start.6
  113.1 0.6 collective-permute-done.25.refs_7_
  113.8 2.5 %shard_map.66.refs_8_ = bf16[256,256]{1,0:T(8,128)(2,1)S(1)} custom-call(s32[2048]{0:T(1024)S(1)} %copy-done.2, s32[8,1,256]{2,1,0:T(1,128)S(1)} %bitcast.1, bf16[256,256]{1,0:T(8,128)(2,1)S(1)} %get-tuple-element.7.q_ref, bf16[256,512]{1,0:T(8,128)(2,1)S(1)} %get-tuple-element.8.refs_0_, bf16[256,512]{1,0:T(8,128)(2,1)S(1)} %collective-permute-done.19.refs_1_, ...), custom_call_target="tpu_custom_call" | custom-call | flops 536870912 | bytes 2097152 | tf_op jit(solution)/shard_map/pallas_call | solution.py:279
  116.3 0.1 collective-permute-start.26
  116.4 3.5 %collective-permute-start.27 = (bf16[256,256]{1,0:T(8,128)(2,1)S(1)}, bf16[256,256]{1,0:T(8,128)(2,1)S(1)}, u32[]{:S(2)}, u32[]{:S(2)}) collective-permute-start(bf16[256,256]{1,0:T(8,128)(2,1)S(1)} %shard_map.66.refs_8_), channel_id=1, source_target_pairs={{0,2},{1,3},{2,0},{3,1},{4,6},{5,7},{6,4},{7,5},{8,10},{9,11},{10,... | collective-permute-start | bytes 393224 | tf_op jit(solution)/shard_map/ppermute | solution.py:27
  119.9 0.4 collective-permute-start.28
  120.3 4.0 %collective-permute-done.26.refs_9_ = bf16[256,256]{1,0:T(8,128)(2,1)S(1)} collective-permute-done((bf16[256,256]{1,0:T(8,128)(2,1)S(1)}, bf16[256,256]{1,0:T(8,128)(2,1)S(1)}, u32[]{:S(2)}, u32[]{:S(2)}) %collective-permute-start.26) | collective-permute-done | bytes 131104 | tf_op jit(solution)/shard_map/ppermute | solution.py:27
  124.3 5.1 %collective-permute-done.27.refs_10_ = bf16[256,256]{1,0:T(8,128)(2,1)S(1)} collective-permute-done((bf16[256,256]{1,0:T(8,128)(2,1)S(1)}, bf16[256,256]{1,0:T(8,128)(2,1)S(1)}, u32[]{:S(2)}, u32[]{:S(2)}) %collective-permute-start.27) | collective-permute-done | bytes 131104 | tf_op jit(solution)/shard_map/ppermute | solution.py:27
  129.4 3.7 %shard_map.67 = bf16[256,1536]{1,0:T(8,128)(2,1)} custom-call(bf16[128,1536]{1,0:T(8,128)(2,1)S(1)} %copy-done.1, bf16[128,1536]{1,0:T(8,128)(2,1)S(1)} %collective-permute-done.refs_1_, bf16[128,1536]{1,0:T(8,128)(2,1)S(1)} %collective-permute-done.1.refs_2_, bf16[128,1536]{1,0:T(8,128)(2,1)S(1)} %collective-permute-done.2.refs_3_, ...), custom_call_target="tpu_custom_call" | custom-call | flops 805306368 | bytes 3670016 | tf_op jit(solution)/shard_map/pallas_call | solution.py:279
  (25 shorter events, 0.1 us)
Async XLA Ops:
  0.0 2.2 %copy-start.3 = (bf16[768,256]{1,0:T(8,128)(2,1)S(1)}, bf16[768,256]{1,0:T(8,128)(2,1)}, u32[]{:S(2)}) copy-start(bf16[768,256]{1,0:T(8,128)(2,1)} %param.10) | copy-start | bytes 1179652
  0.0 33.1 %copy-start = (bf16[256,1536]{1,0:T(8,128)(2,1)S(1)}, bf16[256,1536]{1,0:T(8,128)(2,1)}, u32[]{:S(2)}) copy-start(bf16[256,1536]{1,0:T(8,128)(2,1)} %refs_8_.1) | copy-start | bytes 2359300
  0.0 78.5 %copy-start.1 = (bf16[128,1536]{1,0:T(8,128)(2,1)S(1)}, bf16[128,1536]{1,0:T(8,128)(2,1)}, u32[]{:S(2)}) copy-start(bf16[128,1536]{1,0:T(8,128)(2,1)} %refs_0_.1) | copy-start | bytes 1179652
  2.2 29.3 %collective-permute-start.7 = (bf16[768,768]{1,0:T(8,128)(2,1)S(1)}, bf16[768,768]{1,0:T(8,128)(2,1)S(1)}, u32[]{:S(2)}, u32[]{:S(2)}) collective-permute-start(bf16[768,768]{1,0:T(8,128)(2,1)S(1)} %constant_dynamic-update-slice_fusion.refs_0_), channel_id=1, source_target_pairs={{0,8},{4,20},{8,0},{12,28},{16,24},{20,4},{24,16},{28,12},{1,9},{5... | collective-permute-start | bytes 3538952 | tf_op jit(solution)/shard_map/ppermute | solution.py:27
  5.3 46.6 %collective-permute-start.8 = (bf16[768,768]{1,0:T(8,128)(2,1)S(1)}, bf16[768,768]{1,0:T(8,128)(2,1)S(1)}, u32[]{:S(2)}, u32[]{:S(2)}) collective-permute-start(bf16[768,768]{1,0:T(8,128)(2,1)S(1)} %constant_dynamic-update-slice_fusion.refs_0_), channel_id=1, source_target_pairs={{0,16},{4,12},{8,24},{12,4},{16,0},{20,28},{24,8},{28,20},{1,17},{... | collective-permute-start | bytes 3538952 | tf_op jit(solution)/shard_map/ppermute | solution.py:27
  31.5 20.8 %collective-permute-start.9 = (bf16[768,768]{1,0:T(8,128)(2,1)S(1)}, bf16[768,768]{1,0:T(8,128)(2,1)S(1)}, u32[]{:S(2)}, u32[]{:S(2)}) collective-permute-start(bf16[768,768]{1,0:T(8,128)(2,1)S(1)} %collective-permute-done.7.refs_1_), channel_id=1, source_target_pairs={{0,16},{4,12},{8,24},{12,4},{16,0},{20,28},{24,8},{28,20},{1,17},{... | collective-permute-start | bytes 3538952 | tf_op jit(solution)/shard_map/ppermute | solution.py:27
  33.1 18.0 %collective-permute-start.14 = (bf16[256,1536]{1,0:T(8,128)(2,1)S(1)}, bf16[256,1536]{1,0:T(8,128)(2,1)S(1)}, u32[]{:S(2)}, u32[]{:S(2)}) collective-permute-start(bf16[256,1536]{1,0:T(8,128)(2,1)S(1)} %copy-done), channel_id=1, source_target_pairs={{1,0},{0,1},{3,2},{2,3},{5,4},{4,5},{7,6},{6,7},{9,8},{8,9},{11,10... | collective-permute-start | bytes 2359304 | tf_op jit(solution)/shard_map/ppermute | solution.py:27
  34.8 17.6 %collective-permute-start.10 = (bf16[768,768]{1,0:T(8,128)(2,1)S(1)}, bf16[768,768]{1,0:T(8,128)(2,1)S(1)}, u32[]{:S(2)}, u32[]{:S(2)}) collective-permute-start(bf16[768,768]{1,0:T(8,128)(2,1)S(1)} %constant_dynamic-update-slice_fusion.refs_0_), channel_id=1, source_target_pairs={{0,4},{4,0},{8,12},{12,8},{16,20},{20,16},{24,28},{28,24},{1,5},{5... | collective-permute-start | bytes 3538952 | tf_op jit(solution)/shard_map/ppermute | solution.py:27
  34.8 16.9 %collective-permute-start.16 = (bf16[256,1536]{1,0:T(8,128)(2,1)S(1)}, bf16[256,1536]{1,0:T(8,128)(2,1)S(1)}, u32[]{:S(2)}, u32[]{:S(2)}) collective-permute-start(bf16[256,1536]{1,0:T(8,128)(2,1)S(1)} %copy-done), channel_id=1, source_target_pairs={{2,1},{1,2},{6,5},{5,6},{10,9},{9,10},{14,13},{13,14},{18,17},{17,... | collective-permute-start | bytes 2359304 | tf_op jit(solution)/shard_map/ppermute | solution.py:27
  51.0 2.7 %collective-permute-start.15 = (bf16[256,1536]{1,0:T(8,128)(2,1)S(1)}, bf16[256,1536]{1,0:T(8,128)(2,1)S(1)}, u32[]{:S(2)}, u32[]{:S(2)}) collective-permute-start(bf16[256,1536]{1,0:T(8,128)(2,1)S(1)} %collective-permute-done.14.refs_9_), channel_id=1, source_target_pairs={{2,1},{1,2},{6,5},{5,6},{10,9},{9,10},{14,13},{13,14},{18,17},{17,... | collective-permute-start | bytes 2359304 | tf_op jit(solution)/shard_map/ppermute | solution.py:27
  51.8 28.2 %collective-permute-start.11 = (bf16[768,768]{1,0:T(8,128)(2,1)S(1)}, bf16[768,768]{1,0:T(8,128)(2,1)S(1)}, u32[]{:S(2)}, u32[]{:S(2)}) collective-permute-start(bf16[768,768]{1,0:T(8,128)(2,1)S(1)} %collective-permute-done.7.refs_1_), channel_id=1, source_target_pairs={{0,4},{4,0},{8,12},{12,8},{16,20},{20,16},{24,28},{28,24},{1,5},{5... | collective-permute-start | bytes 3538952 | tf_op jit(solution)/shard_map/ppermute | solution.py:27
  51.8 29.5 %collective-permute-start.12 = (bf16[768,768]{1,0:T(8,128)(2,1)S(1)}, bf16[768,768]{1,0:T(8,128)(2,1)S(1)}, u32[]{:S(2)}, u32[]{:S(2)}) collective-permute-start(bf16[768,768]{1,0:T(8,128)(2,1)S(1)} %collective-permute-done.8.refs_2_), channel_id=1, source_target_pairs={{0,4},{4,0},{8,12},{12,8},{16,20},{20,16},{24,28},{28,24},{1,5},{5... | collective-permute-start | bytes 3538952 | tf_op jit(solution)/shard_map/ppermute | solution.py:27
  52.3 29.0 %collective-permute-start.13 = (bf16[768,768]{1,0:T(8,128)(2,1)S(1)}, bf16[768,768]{1,0:T(8,128)(2,1)S(1)}, u32[]{:S(2)}, u32[]{:S(2)}) collective-permute-start(bf16[768,768]{1,0:T(8,128)(2,1)S(1)} %collective-permute-done.9.refs_3_), channel_id=1, source_target_pairs={{0,4},{4,0},{8,12},{12,8},{16,20},{20,16},{24,28},{28,24},{1,5},{5... | collective-permute-start | bytes 3538952 | tf_op jit(solution)/shard_map/ppermute | solution.py:27
  52.4 26.1 %collective-permute-start.17 = (bf16[256,1536]{1,0:T(8,128)(2,1)S(1)}, bf16[256,1536]{1,0:T(8,128)(2,1)S(1)}, u32[]{:S(2)}, u32[]{:S(2)}) collective-permute-start(bf16[256,1536]{1,0:T(8,128)(2,1)S(1)} %collective-permute-done.16.refs_11_), channel_id=1, source_target_pairs={{1,0},{2,3},{5,4},{6,7},{9,8},{10,11},{13,12},{14,15},{17,16},{18,... | collective-permute-start | bytes 2359304 | tf_op jit(solution)/shard_map/ppermute | solution.py:27
  53.7 41.4 %collective-permute-start.18 = (bf16[256,1536]{1,0:T(8,128)(2,1)S(1)}, bf16[256,1536]{1,0:T(8,128)(2,1)S(1)}, u32[]{:S(2)}, u32[]{:S(2)}) collective-permute-start(bf16[256,1536]{1,0:T(8,128)(2,1)S(1)} %collective-permute-done.15.refs_10_), channel_id=1, source_target_pairs={{1,0},{2,3},{5,4},{6,7},{9,8},{10,11},{13,12},{14,15},{17,16},{18,... | collective-permute-start | bytes 2359304 | tf_op jit(solution)/shard_map/ppermute | solution.py:27
  78.5 21.0 %collective-permute-start = (bf16[128,1536]{1,0:T(8,128)(2,1)S(1)}, bf16[128,1536]{1,0:T(8,128)(2,1)S(1)}, u32[]{:S(2)}, u32[]{:S(2)}) collective-permute-start(bf16[128,1536]{1,0:T(8,128)(2,1)S(1)} %copy-done.1), channel_id=1, source_target_pairs={{0,8},{4,20},{8,0},{12,28},{16,24},{20,4},{24,16},{28,12},{1,9},{5... | collective-permute-start | bytes 1179656 | tf_op jit(solution)/shard_map/ppermute | solution.py:27
  80.0 27.2 %collective-permute-start.1 = (bf16[128,1536]{1,0:T(8,128)(2,1)S(1)}, bf16[128,1536]{1,0:T(8,128)(2,1)S(1)}, u32[]{:S(2)}, u32[]{:S(2)}) collective-permute-start(bf16[128,1536]{1,0:T(8,128)(2,1)S(1)} %copy-done.1), channel_id=1, source_target_pairs={{0,16},{4,12},{8,24},{12,4},{16,0},{20,28},{24,8},{28,20},{1,17},{... | collective-permute-start | bytes 1179656 | tf_op jit(solution)/shard_map/ppermute | solution.py:27
  86.0 27.8 %copy-start.2 = (s32[2048]{0:T(1024)S(1)}, s32[2048]{0:T(1024)}, u32[]{:S(2)}) copy-start(s32[2048]{0:T(1024)} %ids.1) | copy-start | bytes 24580
  96.6 9.2 %collective-permute-start.19 = (bf16[256,512]{1,0:T(8,128)(2,1)S(1)}, bf16[256,512]{1,0:T(8,128)(2,1)S(1)}, u32[]{:S(2)}, u32[]{:S(2)}) collective-permute-start(bf16[256,512]{1,0:T(8,128)(2,1)S(1)} %get-tuple-element.8.refs_0_), channel_id=1, source_target_pairs={{0,8},{4,20},{8,0},{12,28},{16,24},{20,4},{24,16},{28,12},{1,9},{5... | collective-permute-start | bytes 786440 | tf_op jit(solution)/shard_map/ppermute | solution.py:27
  98.1 9.0 %collective-permute-start.20 = (bf16[256,512]{1,0:T(8,128)(2,1)S(1)}, bf16[256,512]{1,0:T(8,128)(2,1)S(1)}, u32[]{:S(2)}, u32[]{:S(2)}) collective-permute-start(bf16[256,512]{1,0:T(8,128)(2,1)S(1)} %get-tuple-element.8.refs_0_), channel_id=1, source_target_pairs={{0,16},{4,12},{8,24},{12,4},{16,0},{20,28},{24,8},{28,20},{1,17},{... | collective-permute-start | bytes 786440 | tf_op jit(solution)/shard_map/ppermute | solution.py:27
  99.5 9.5 %collective-permute-start.2 = (bf16[128,1536]{1,0:T(8,128)(2,1)S(1)}, bf16[128,1536]{1,0:T(8,128)(2,1)S(1)}, u32[]{:S(2)}, u32[]{:S(2)}) collective-permute-start(bf16[128,1536]{1,0:T(8,128)(2,1)S(1)} %collective-permute-done.refs_1_), channel_id=1, source_target_pairs={{0,16},{4,12},{8,24},{12,4},{16,0},{20,28},{24,8},{28,20},{1,17},{... | collective-permute-start | bytes 1179656 | tf_op jit(solution)/shard_map/ppermute | solution.py:27
  100.2 9.9 %collective-permute-start.22 = (bf16[256,512]{1,0:T(8,128)(2,1)S(1)}, bf16[256,512]{1,0:T(8,128)(2,1)S(1)}, u32[]{:S(2)}, u32[]{:S(2)}) collective-permute-start(bf16[256,512]{1,0:T(8,128)(2,1)S(1)} %get-tuple-element.8.refs_0_), channel_id=1, source_target_pairs={{0,4},{4,0},{8,12},{12,8},{16,20},{20,16},{24,28},{28,24},{1,5},{5... | collective-permute-start | bytes 786440 | tf_op jit(solution)/shard_map/ppermute | solution.py:27
  105.8 6.4 %collective-permute-start.21 = (bf16[256,512]{1,0:T(8,128)(2,1)S(1)}, bf16[256,512]{1,0:T(8,128)(2,1)S(1)}, u32[]{:S(2)}, u32[]{:S(2)}) collective-permute-start(bf16[256,512]{1,0:T(8,128)(2,1)S(1)} %collective-permute-done.19.refs_1_), channel_id=1, source_target_pairs={{0,16},{4,12},{8,24},{12,4},{16,0},{20,28},{24,8},{28,20},{1,17},{... | collective-permute-start | bytes 786440 | tf_op jit(solution)/shard_map/ppermute | solution.py:27
  107.1 5.5 %collective-permute-start.23 = (bf16[256,512]{1,0:T(8,128)(2,1)S(1)}, bf16[256,512]{1,0:T(8,128)(2,1)S(1)}, u32[]{:S(2)}, u32[]{:S(2)}) collective-permute-start(bf16[256,512]{1,0:T(8,128)(2,1)S(1)} %collective-permute-done.19.refs_1_), channel_id=1, source_target_pairs={{0,4},{4,0},{8,12},{12,8},{16,20},{20,16},{24,28},{28,24},{1,5},{5... | collective-permute-start | bytes 786440 | tf_op jit(solution)/shard_map/ppermute | solution.py:27
  107.1 5.6 %collective-permute-start.24 = (bf16[256,512]{1,0:T(8,128)(2,1)S(1)}, bf16[256,512]{1,0:T(8,128)(2,1)S(1)}, u32[]{:S(2)}, u32[]{:S(2)}) collective-permute-start(bf16[256,512]{1,0:T(8,128)(2,1)S(1)} %collective-permute-done.20.refs_2_), channel_id=1, source_target_pairs={{0,4},{4,0},{8,12},{12,8},{16,20},{20,16},{24,28},{28,24},{1,5},{5... | collective-permute-start | bytes 786440 | tf_op jit(solution)/shard_map/ppermute | solution.py:27
  108.9 7.4 %collective-permute-start.3 = (bf16[128,1536]{1,0:T(8,128)(2,1)S(1)}, bf16[128,1536]{1,0:T(8,128)(2,1)S(1)}, u32[]{:S(2)}, u32[]{:S(2)}) collective-permute-start(bf16[128,1536]{1,0:T(8,128)(2,1)S(1)} %copy-done.1), channel_id=1, source_target_pairs={{0,4},{4,0},{8,12},{12,8},{16,20},{20,16},{24,28},{28,24},{1,5},{5... | collective-permute-start | bytes 1179656 | tf_op jit(solution)/shard_map/ppermute | solution.py:27
  110.1 9.8 %collective-permute-start.4 = (bf16[128,1536]{1,0:T(8,128)(2,1)S(1)}, bf16[128,1536]{1,0:T(8,128)(2,1)S(1)}, u32[]{:S(2)}, u32[]{:S(2)}) collective-permute-start(bf16[128,1536]{1,0:T(8,128)(2,1)S(1)} %collective-permute-done.refs_1_), channel_id=1, source_target_pairs={{0,4},{4,0},{8,12},{12,8},{16,20},{20,16},{24,28},{28,24},{1,5},{5... | collective-permute-start | bytes 1179656 | tf_op jit(solution)/shard_map/ppermute | solution.py:27
  112.2 1.6 %collective-permute-start.25 = (bf16[256,512]{1,0:T(8,128)(2,1)S(1)}, bf16[256,512]{1,0:T(8,128)(2,1)S(1)}, u32[]{:S(2)}, u32[]{:S(2)}) collective-permute-start(bf16[256,512]{1,0:T(8,128)(2,1)S(1)} %collective-permute-done.21.refs_3_), channel_id=1, source_target_pairs={{0,4},{4,0},{8,12},{12,8},{16,20},{20,16},{24,28},{28,24},{1,5},{5... | collective-permute-start | bytes 786440 | tf_op jit(solution)/shard_map/ppermute | solution.py:27
  112.6 7.7 %collective-permute-start.5 = (bf16[128,1536]{1,0:T(8,128)(2,1)S(1)}, bf16[128,1536]{1,0:T(8,128)(2,1)S(1)}, u32[]{:S(2)}, u32[]{:S(2)}) collective-permute-start(bf16[128,1536]{1,0:T(8,128)(2,1)S(1)} %collective-permute-done.1.refs_2_), channel_id=1, source_target_pairs={{0,4},{4,0},{8,12},{12,8},{16,20},{20,16},{24,28},{28,24},{1,5},{5... | collective-permute-start | bytes 1179656 | tf_op jit(solution)/shard_map/ppermute | solution.py:27
  112.7 7.5 %collective-permute-start.6 = (bf16[128,1536]{1,0:T(8,128)(2,1)S(1)}, bf16[128,1536]{1,0:T(8,128)(2,1)S(1)}, u32[]{:S(2)}, u32[]{:S(2)}) collective-permute-start(bf16[128,1536]{1,0:T(8,128)(2,1)S(1)} %collective-permute-done.2.refs_3_), channel_id=1, source_target_pairs={{0,4},{4,0},{8,12},{12,8},{16,20},{20,16},{24,28},{28,24},{1,5},{5... | collective-permute-start | bytes 1179656 | tf_op jit(solution)/shard_map/ppermute | solution.py:27
  116.3 7.9 %collective-permute-start.26 = (bf16[256,256]{1,0:T(8,128)(2,1)S(1)}, bf16[256,256]{1,0:T(8,128)(2,1)S(1)}, u32[]{:S(2)}, u32[]{:S(2)}) collective-permute-start(bf16[256,256]{1,0:T(8,128)(2,1)S(1)} %shard_map.66.refs_8_), channel_id=1, source_target_pairs={{0,1},{1,2},{2,3},{3,0},{4,5},{5,6},{6,7},{7,4},{8,9},{9,10},{10,1... | collective-permute-start | bytes 393224 | tf_op jit(solution)/shard_map/ppermute | solution.py:27
  116.4 13.0 %collective-permute-start.27 = (bf16[256,256]{1,0:T(8,128)(2,1)S(1)}, bf16[256,256]{1,0:T(8,128)(2,1)S(1)}, u32[]{:S(2)}, u32[]{:S(2)}) collective-permute-start(bf16[256,256]{1,0:T(8,128)(2,1)S(1)} %shard_map.66.refs_8_), channel_id=1, source_target_pairs={{0,2},{1,3},{2,0},{3,1},{4,6},{5,7},{6,4},{7,5},{8,10},{9,11},{10,... | collective-permute-start | bytes 393224 | tf_op jit(solution)/shard_map/ppermute | solution.py:27
  119.9 9.5 %collective-permute-start.28 = (bf16[256,256]{1,0:T(8,128)(2,1)S(1)}, bf16[256,256]{1,0:T(8,128)(2,1)S(1)}, u32[]{:S(2)}, u32[]{:S(2)}) collective-permute-start(bf16[256,256]{1,0:T(8,128)(2,1)S(1)} %shard_map.66.refs_8_), channel_id=1, source_target_pairs={{0,3},{1,0},{2,1},{3,2},{4,7},{5,4},{6,5},{7,6},{8,11},{9,8},{10,9... | collective-permute-start | bytes 393224 | tf_op jit(solution)/shard_map/ppermute | solution.py:27
